TPU v7x, 512 devices: a whole 4x4x16 slice. The times are simulated.
512 devices in a mesh: ctx: 16 (over x, z_hi, core), head: 32 (over z_lo, y).
Axes of the slice: x: 4, y: 4, z: 16 (z_hi: 2, z_lo: 8; z = z_hi * 8 + z_lo), core: 2. Of those that a mesh axis runs over, the one named last changes fastest.
Arguments:
- q_nope: bfloat16 [2048, 128, 128], P('ctx', 'head'), may hold values from -6 to 6
- q_rope: bfloat16 [2048, 128, 64], P('ctx', 'head'), may hold values from -300 to 300
- w_uk: bfloat16 [128, 128, 512], P('head'), may hold values from -0.5 to 0.5
- w_uv: bfloat16 [128, 512, 128], P('head'), may hold values from -0.75 to 0.75
- w_o: bfloat16 [16384, 7168], P('head', 'ctx'), may hold values from -0.125 to 0.125
- cache_kv: bfloat16 [2048, 576], P('ctx'), may hold values from -4 to 4
- new_kv: bfloat16 [2048, 576], P('ctx'), may hold values from -4 to 4
- block_order: int32 [16], replicated, may hold values from 0 to 15, each once
- cache_lengths: int32 [16], replicated, may hold values from 32 to 128, as said below
Outputs:
- mixed: bfloat16 [2048, 7168], P(('ctx', 'head'))
Inputs may be any that keep to these rules, and one draw needn't show every extreme that they name: `cache_lengths`: at least one ctx index has all 128 slots valid.
All inputs are finite; a program needn't handle non-finite values.
Results may differ from a plain program's by a relative error of at most 0.024.
Values may be sent and summed in bfloat16 or wider, within the bound.
No kernel may reach another device: no remote copies, remote signals or barrier semaphores. Data moves between devices by JAX's collectives and lax.ppermute only.
A program may use at most 64 MiB of HBM per device.

v0:
```python
import jax
import jax.numpy as jnp
from jax import lax
from jax.sharding import PartitionSpec as P

neg_large = -1e30


def on_device(q_nope, q_rope, w_uk, w_uv, w_o, cache_kv, new_kv, block_order, cache_lengths):
    tok_rows, heads_here, nope_width = q_nope.shape
    latent_width = w_uk.shape[2]
    value_width = w_uv.shape[2]
    cache_rows = cache_kv.shape[0]
    shard_rows = cache_rows + tok_rows
    ctx_count = lax.axis_size("ctx")
    score_scale = float(nope_width + q_rope.shape[2]) ** (-0.5)
    query_rows = tok_rows * heads_here
    q_latent = jnp.einsum("thn,hnc->thc", q_nope, w_uk, preferred_element_type=jnp.float32)
    query = jnp.concatenate([q_latent, q_rope.astype(jnp.float32)], axis=2).astype(jnp.bfloat16)
    query = query.reshape(query_rows, query.shape[2])
    shard_ids = jnp.arange(ctx_count, dtype=jnp.int32)
    own_block = jnp.sum(jnp.where(shard_ids == lax.axis_index("ctx"), block_order, 0))
    query_pos = own_block * tok_rows + jnp.arange(query_rows, dtype=jnp.int32) // heads_here
    local_keys = jnp.concatenate([cache_kv, new_kv], axis=0)
    piece = lax.all_gather(local_keys, "ctx", axis=0, tiled=True)
    global_rows = jnp.arange(piece.shape[0], dtype=jnp.int32)
    owners = global_rows // shard_rows
    offsets = global_rows % shard_rows
    matches = owners[:, None] == shard_ids[None, :]
    lengths = jnp.sum(jnp.where(matches, cache_lengths[None, :], 0), axis=1)
    blocks = jnp.sum(jnp.where(matches, block_order[None, :], 0), axis=1)
    key_pos = blocks * tok_rows + offsets - cache_rows
    visible = jnp.where(
        (offsets < cache_rows)[None, :],
        (offsets < lengths)[None, :],
        key_pos[None, :] <= query_pos[:, None],
    )
    best = jnp.full((query_rows,), neg_large, jnp.float32)
    scores = (
        lax.dot_general(query, piece, (((1,), (1,)), ((), ())), preferred_element_type=jnp.float32)
        * score_scale
    )
    fresh = jnp.maximum(best, jnp.max(jnp.where(visible, scores, neg_large), axis=1))
    expo = jnp.where(visible, jnp.exp(scores - fresh[:, None]), 0.0)
    totals = jnp.sum(expo, axis=1)
    accum = jnp.dot(
        expo.astype(jnp.bfloat16), piece[:, :latent_width], preferred_element_type=jnp.float32
    )
    best, totals, accum = (fresh, totals, accum)
    latent_out = (
        (accum / totals[:, None]).astype(jnp.bfloat16).reshape(tok_rows, heads_here, latent_width)
    )
    head_out = jnp.einsum("thc,hcv->thv", latent_out, w_uv, preferred_element_type=jnp.float32)
    head_out = head_out.astype(jnp.bfloat16).reshape(tok_rows, heads_here * value_width)
    partial_cols = jnp.dot(
        head_out, lax.all_gather(w_o, "ctx", axis=1, tiled=True), preferred_element_type=jnp.float32
    )
    return lax.psum_scatter(
        partial_cols.astype(jnp.bfloat16), "head", scatter_dimension=0, tiled=True
    )


def solution(mesh):
    in_specs = (
        P("ctx", "head", None),
        P("ctx", "head", None),
        P("head", None, None),
        P("head", None, None),
        P("head", "ctx"),
        P("ctx", None),
        P("ctx", None),
        P(),
        P(),
    )
    out_specs = P(("ctx", "head"), None)
    return jax.shard_map(
        on_device, mesh=mesh, in_specs=in_specs, out_specs=out_specs, check_vma=False
    )
```

profile of v0, /device:TPU:6, one launch (start us, length us, event | category | flops | bytes accessed | tf_op | source)
XLA Modules:
  0.0 768.2 jit_solution(10185710093773951270)
XLA Ops:
  6.5 0.0 copy-start
  6.5 0.0 all-gather.3.cloned.1.call-start
  6.5 1.8 pad_maximum_fusion
  8.3 0.0 all-gather.3.cloned.1.call-update
  8.4 0.0 all-gather.5.cloned.1.call-start
  8.4 0.7 all-gather.5.cloned.1.call-update
  9.1 0.0 all-reduce.3.cloned.1.call-start
  9.2 0.0 copy-done
  9.2 1.2 fusion.11
  10.4 0.4 copy.24
  10.8 0.1 concatenate.12
  10.9 1.0 copy.25
  11.9 1.3 fusion.33
  13.9 0.8 select_reduce_fusion.2
  14.7 127.3 %all-gather.3.cloned.1.call-done = bf16[4096,576]{0,1:T(8,128)(2,1)} async-done(((bf16[256,576]{0,1:T(8,128)(2,1)}), bf16[4096,576]{0,1:T(8,128)(2,1)}) %all-gather.3.cloned.1.call-update) | async-done | bytes 4718608 | tf_op jit(solution)/shard_map/all_gather | solution.py:25
  142.0 0.0 slice-start
  142.0 0.0 slice-start.1
  142.0 6.4 select_reduce_fusion
  148.5 3.5 fusion
  152.0 0.0 slice-done
  152.0 0.0 slice-done.1
  152.0 0.0 copy-start.1
  152.0 2.9 divide_convert_fusion
  154.9 0.1 reshape.66
  155.0 0.0 copy-done.1
  155.1 0.4 convolution_convert_fusion.2
  155.4 145.6 %all-gather.5.cloned.1.call-done = bf16[512,7168]{0,1:T(8,128)(2,1)} async-done(((bf16[512,448]{0,1:T(8,128)(2,1)}), bf16[512,7168]{0,1:T(8,128)(2,1)}) %all-gather.5.cloned.1.call-update) | async-done | bytes 7340048 | tf_op jit(solution)/shard_map/all_gather | solution.py:56
  301.0 6.9 convolution_convert_fusion
  307.9 0.0 all-reduce.3.cloned.1.call-update
  307.9 1.3 dynamic-slice
  309.9 450.3 %all-reduce.3.cloned.1.call-done = bf16[128,7168]{1,0:T(8,128)(2,1)} async-done(((bf16[128,7168]{1,0:T(8,128)(2,1)}), bf16[128,7168]{1,0:T(8,128)(2,1)}) %all-reduce.3.cloned.1.call-update) | async-done | bytes 1835024
  760.1 1.6 constant_dynamic-slice_fusion
  (6 shorter events, 0.0 us)
Async XLA Ops:
  6.5 2.6 copy-start
  6.5 135.5 %all-gather.3.cloned.1.call-start = ((), (), s32[]{:S(2)}) async-start(), calls=%async_computation | async-start | bytes 5013504 | tf_op jit(solution)/shard_map/all_gather | solution.py:25
  8.4 292.7 %all-gather.5.cloned.1.call-start = ((), (), s32[]{:S(2)}) async-start(), calls=%async_computation.1 | async-start | bytes 7798784 | tf_op jit(solution)/shard_map/all_gather | solution.py:56
  9.1 751.0 %all-reduce.3.cloned.1.call-start = ((), (), s32[]{:S(2)}) async-start(), calls=%async_computation.2 | async-start | bytes 3670016
  142.0 10.0 %slice-start = ((s8[4718592]{0:T(1024)(128)(4,1)}), s8[4194304]{0:T(1024)(128)(4,1)S(1)}, s32[]{:S(2)}) async-start(s8[4718592]{0:T(1024)(128)(4,1)} %bitcast.14), calls=%async_computation.3 | async-start | bytes 8388608
  142.0 10.0 %slice-start.1 = ((s8[4718592]{0:T(1024)(128)(4,1)}), s8[524288]{0:T(1024)(128)(4,1)S(1)}, s32[]{:S(2)}) async-start(s8[4718592]{0:T(1024)(128)(4,1)} %bitcast.14), calls=%async_computation.4 | async-start | bytes 1048576
  152.0 3.0 copy-start.1
Sparse Core Ops, SparseCore 0:
  10.5 131.5 all-gather.2
  145.3 155.6 all-gather.4
  308.1 452.0 all-reduce.2
where the time goes:
time: 769 us; the launch traced here: 768 us
  waiting for transfers between devices  724 us (94%)
  matrix products  17.7 us (2%)
  between operations  14.6 us (2%)
    unnamed x4, waiting for transfers between devices  451 us
    all_gather x1, waiting for transfers between devices, on_device(): lax.all_gather(w_o, 'ctx', axis=1, tiled=True)  146 us
    all_gather x1, waiting for transfers between devices, on_device(): piece = lax.all_gather(local_keys, 'ctx', axis=0, tiled=True)  127 us
  transfers between devices with their start and end apart: 3, of which 3 were waited for; matrix products, arithmetic and copies ran while one was open for 3% of the time, Pallas kernels for 0%

commit v1 on v0

v1 whole, which is shorter than its diff:
```python
import jax
import jax.numpy as jnp
from jax import lax
from jax.sharding import Mesh
from jax.sharding import PartitionSpec as P

neg_large = -1e30
f32 = jnp.float32
bf16 = jnp.bfloat16


def spread(value, axes):
    count = lax.axis_size(axes)
    copies = jnp.broadcast_to(value[None], (count,) + value.shape)
    return lax.all_to_all(copies, axes, 0, 0, tiled=False)


def on_device(q_nope, q_rope, w_uk, w_uv, w_o, cache_kv, new_kv, block_order, cache_lengths):
    tok_rows, heads_here, nope_width = q_nope.shape
    latent_width = w_uk.shape[2]
    value_width = w_uv.shape[2]
    key_width = cache_kv.shape[1]
    cache_rows = cache_kv.shape[0]
    shard_rows = cache_rows + tok_rows
    x_size, zh_size, core_size = (lax.axis_size(a) for a in ("x", "zh", "core"))
    zl_size, y_size = lax.axis_size("zl"), lax.axis_size("y")
    x_at, zh_at, core_at, zl_at, y_at = (lax.axis_index(a) for a in ("x", "zh", "core", "zl", "y"))
    score_scale = float(nope_width + q_rope.shape[2]) ** (-0.5)
    query_rows = tok_rows * heads_here

    swap_zh = [(0, 1), (1, 0)]
    mirror = [(i, zh_size * zl_size - 1 - i) for i in range(zh_size * zl_size)]

    local_keys = jnp.concatenate([cache_kv, new_kv], axis=0)
    quarter_rows = shard_rows // y_size
    quarter = lax.dynamic_slice_in_dim(local_keys, y_at * quarter_rows, quarter_rows, 0)
    far_quarter = lax.ppermute(quarter, ("zh", "zl"), mirror)

    value_rows, col_count = w_o.shape
    cols = col_count // y_size
    w_t = w_o.T.reshape(y_size, cols, value_rows)
    w_t = lax.all_to_all(w_t, "y", 0, 0, tiled=False)
    w_t = jnp.transpose(w_t, (1, 0, 2))

    near = spread(local_keys, "x")
    far = spread(far_quarter, ("x", "y"))
    far = far.reshape(x_size, shard_rows, key_width)
    w_far = lax.ppermute(w_t, "zh", swap_zh)
    half = jnp.stack([near, far])
    other_half = lax.ppermute(half, "core", swap_zh)
    piece = jnp.stack([half, other_half])
    piece = piece.reshape(-1, key_width)

    w_pair = jnp.where(zh_at == 0, jnp.stack([w_t, w_far]), jnp.stack([w_far, w_t]))
    w_pair_other = lax.ppermute(w_pair, "core", swap_zh)
    w_all = jnp.where(
        core_at == 0,
        jnp.stack([w_pair, w_pair_other], axis=1),
        jnp.stack([w_pair_other, w_pair], axis=1),
    )
    w_all = w_all.reshape(zh_size * core_size * cols, y_size * value_rows)

    q_latent = jnp.einsum("thn,hnc->thc", q_nope, w_uk, preferred_element_type=f32)
    query = jnp.concatenate([q_latent, q_rope.astype(f32)], axis=2).astype(bf16)
    query = query.reshape(query_rows, query.shape[2])
    ctx_count = x_size * zh_size * core_size
    shard_ids = jnp.arange(ctx_count, dtype=jnp.int32)
    own_ctx = (x_at * zh_size + zh_at) * core_size + core_at
    own_block = jnp.sum(jnp.where(shard_ids == own_ctx, block_order, 0))
    query_pos = own_block * tok_rows + jnp.arange(query_rows, dtype=jnp.int32) // heads_here

    global_rows = jnp.arange(piece.shape[0], dtype=jnp.int32)
    part = global_rows // shard_rows
    offsets = global_rows % shard_rows
    part_x = part % x_size
    part_zh = (part // x_size % zh_size) ^ zh_at
    part_core = (part // (x_size * zh_size)) ^ core_at
    owners = (part_x * zh_size + part_zh) * core_size + part_core
    matches = owners[:, None] == shard_ids[None, :]
    lengths = jnp.sum(jnp.where(matches, cache_lengths[None, :], 0), axis=1)
    blocks = jnp.sum(jnp.where(matches, block_order[None, :], 0), axis=1)
    key_pos = blocks * tok_rows + offsets - cache_rows
    visible = jnp.where(
        (offsets < cache_rows)[None, :],
        (offsets < lengths)[None, :],
        key_pos[None, :] <= query_pos[:, None],
    )
    scores = (
        lax.dot_general(query, piece, (((1,), (1,)), ((), ())), preferred_element_type=f32)
        * score_scale
    )
    best = jnp.max(jnp.where(visible, scores, neg_large), axis=1)
    expo = jnp.where(visible, jnp.exp(scores - best[:, None]), 0.0)
    totals = jnp.sum(expo, axis=1)
    accum = jnp.dot(expo.astype(bf16), piece[:, :latent_width], preferred_element_type=f32)
    latent_out = (accum / totals[:, None]).astype(bf16).reshape(tok_rows, heads_here, latent_width)
    head_out = jnp.einsum("thc,hcv->thv", latent_out, w_uv, preferred_element_type=f32)
    head_out = head_out.astype(bf16).reshape(tok_rows, heads_here * value_width)

    gathered = spread(head_out, ("x", "y"))
    gathered = gathered.reshape(x_size, y_size, zl_size, tok_rows // zl_size, value_rows)
    lhs = jnp.transpose(gathered, (2, 0, 3, 1, 4)).reshape(x_size * tok_rows, y_size * value_rows)
    partial = lax.dot_general(lhs, w_all, (((1,), (1,)), ((), ())), preferred_element_type=f32)
    partial = partial.astype(bf16)

    step = 1
    pieces = partial.reshape(2, 2, 2, -1, partial.shape[1])
    for axis, bit in ((2, 1), (1, 2), (0, 4)):
        mine = (zl_at // bit) % 2
        keep = lax.dynamic_index_in_dim(pieces, mine, axis, keepdims=True)
        send = lax.dynamic_index_in_dim(pieces, 1 - mine, axis, keepdims=True)
        got = lax.ppermute(send, "zl", [(i, i ^ bit) for i in range(zl_size)])
        pieces = (keep.astype(f32) + got.astype(f32)).astype(bf16)
    rows_out = tok_rows // (zl_size * y_size)
    summed = pieces.reshape(x_size * y_size, rows_out, partial.shape[1])
    mixed = lax.all_to_all(summed, ("x", "y"), 0, 0, tiled=False)
    mixed = mixed.reshape(x_size, y_size, rows_out, zh_size * core_size, cols)
    mixed = jnp.transpose(mixed, (2, 0, 3, 1, 4))
    return mixed.reshape(rows_out, x_size * zh_size * core_size * y_size * cols)


def solution(mesh):
    axes = ("x", "zh", "core", "zl", "y")
    fine = Mesh(mesh.devices.reshape(4, 2, 2, 8, 4), axes)
    ctx, head = axes[:3], axes[3:]
    in_specs = (
        P(ctx, head, None),
        P(ctx, head, None),
        P(head, None, None),
        P(head, None, None),
        P(head, ctx),
        P(ctx, None),
        P(ctx, None),
        P(),
        P(),
    )
    out_specs = P(axes, None)
    return jax.shard_map(
        on_device, mesh=fine, in_specs=in_specs, out_specs=out_specs, check_vma=False
    )
```

time: 769 us -> 218 us (0.28)
  waiting for transfers between devices: 724 us -> 98.2 us
  starting transfers between devices: 0.08 us -> 55.2 us
  local copies, waits for them, and re-layouts: 4.47 us -> 23.8 us
  between operations: 14.6 us -> 1.15 us
  blocking collectives: 0 us -> 12.7 us
  matrix products: 17.7 us -> 8.37 us
  other arithmetic: 7.5 us -> 16.1 us
    unnamed x4 -> x0, waiting for transfers between devices: 451 us -> none
    all_gather x2 -> x0, waiting for transfers between devices: 273 us -> none  [the longest x1 146 us: on_device(): lax.all_gather(w_o, 'ctx', axis=1, tiled=True)]
    ppermute x0 -> x7, waiting for transfers between devices: none -> 81.6 us  [the longest x1 43.3 us: on_device(): w_far = lax.ppermute(w_t, 'zh', swap_zh)]
    all_to_all x0 -> x4, starting transfers between devices: none -> 28.3 us  [the longest x3 24.2 us: spread(): return lax.all_to_all(copies, axes, 0, 0, tiled=False)]
    ppermute x0 -> x7, starting transfers between devices: none -> 26.9 us  [the longest x1 8.21 us: on_device(): w_far = lax.ppermute(w_t, 'zh', swap_zh)]
    all_to_all x0 -> x4, waiting for transfers between devices: none -> 16.6 us  [the longest x3 16.6 us: spread(): return lax.all_to_all(copies, axes, 0, 0, tiled=False)]
    all_to_all x0 -> x1, blocking collectives: none -> 12.7 us  [on_device(): mixed = lax.all_to_all(summed, ('x', 'y'), 0, 0, tiled=False)]
  transfers between devices with their start and end apart: 3 -> 11, of which waited for: 3 -> 7; matrix products, arithmetic and copies ran while one was open for 3% -> 14% of each run, Pallas kernels for 0% -> 0%
where the time goes in v1:
time: 218 us; the launch traced here: 216 us
  waiting for transfers between devices  98.2 us (45%)
  starting transfers between devices  55.2 us (25%)
  local copies, waits for them, and re-layouts  23.8 us (11%)
  other arithmetic  16.1 us (7%)
  blocking collectives  12.7 us (6%)
  matrix products  8.37 us (4%)
    ppermute x1, waiting for transfers between devices, on_device(): w_far = lax.ppermute(w_t, 'zh', swap_zh)  43.3 us
    ppermute x3, waiting for transfers between devices, on_device(): got = lax.ppermute(send, 'zl', [(i, i ^ bit) for i in range(zl_size)])  24.3 us
    all_to_all x3, starting transfers between devices, spread(): return lax.all_to_all(copies, axes, 0, 0, tiled=False)  24.2 us
    all_to_all x3, waiting for transfers between devices, spread(): return lax.all_to_all(copies, axes, 0, 0, tiled=False)  16.6 us
    ppermute x1, waiting for transfers between devices, on_device(): far_quarter = lax.ppermute(quarter, ('zh', 'zl'), mirror)  12.8 us
    all_to_all x1, blocking collectives, on_device(): mixed = lax.all_to_all(summed, ('x', 'y'), 0, 0, tiled=False)  12.7 us
    ppermute x1, starting transfers between devices, on_device(): w_far = lax.ppermute(w_t, 'zh', swap_zh)  8.21 us
    ppermute x3, starting transfers between devices, on_device(): got = lax.ppermute(send, 'zl', [(i, i ^ bit) for i in range(zl_size)])  7.67 us
  transfers between devices with their start and end apart: 11, of which 7 were waited for; matrix products, arithmetic and copies ran while one was open for 14% of the time, Pallas kernels for 0%

profile of v1, /device:TPU:6, one launch (start us, length us, event | category | flops | bytes accessed | tf_op | source)
XLA Modules:
  0.0 215.5 jit_solution(10611165408550106925)
XLA Ops:
  3.1 9.3 %all-to-all-start = ((bf16[4,256,576]{1,2,0:T(8,128)(2,1)}), bf16[4,256,576]{1,2,0:T(8,128)(2,1)S(1)}, u32[]{:S(2)}, u32[]{:S(2)}) async-start(bf16[4,256,576]{1,2,0:T(8,128)(2,1)} %broadcast_in_dim.80), calls=%async_computation | async-start | bytes 2359296 | tf_op jit(solution)/shard_map/all_to_all | solution.py:15
  12.5 6.8 %collective-permute-start = (bf16[64,576]{0,1:T(8,128)(2,1)S(1)}, bf16[64,576]{0,1:T(8,128)(2,1)S(1)}, u32[]{:S(2)}, u32[]{:S(2)}) collective-permute-start(bf16[64,576]{0,1:T(8,128)(2,1)S(1)} %constant_dynamic-slice_fusion.2), channel_id=1, source_target_pairs={{0,92},{4,88},{8,84},{12,80},{16,76},{20,72},{24,68},{28,64},{64,2... | collective-permute-start | bytes 221192 | tf_op jit(solution)/shard_map/ppermute | solution.py:37
  19.4 12.8 %collective-permute-done = bf16[64,576]{0,1:T(8,128)(2,1)S(1)} collective-permute-done((bf16[64,576]{0,1:T(8,128)(2,1)S(1)}, bf16[64,576]{0,1:T(8,128)(2,1)S(1)}, u32[]{:S(2)}, u32[]{:S(2)}) %collective-permute-start) | collective-permute-done | bytes 73760 | tf_op jit(solution)/shard_map/ppermute | solution.py:37
  33.5 7.5 %all-to-all-start.1 = ((bf16[16,64,576]{2,1,0:T(8,128)(2,1)}), bf16[16,64,576]{2,1,0:T(8,128)(2,1)S(1)}, u32[]{:S(2)}, u32[]{:S(2)}) async-start(bf16[16,64,576]{2,1,0:T(8,128)(2,1)} %broadcast_in_dim.81), calls=%async_computation.1 | async-start | bytes 2621440 | tf_op jit(solution)/shard_map/all_to_all | solution.py:15
  40.9 1.4 copy.71
  42.4 16.6 %all-to-all-done.1 = bf16[16,64,576]{2,1,0:T(8,128)(2,1)S(1)} async-done(((bf16[16,64,576]{2,1,0:T(8,128)(2,1)}), bf16[16,64,576]{2,1,0:T(8,128)(2,1)S(1)}, u32[]{:S(2)}, u32[]{:S(2)}) %all-to-all-start.1) | async-done | bytes 1179680 | tf_op jit(solution)/shard_map/all_to_all | solution.py:15
  60.1 3.7 %fusion.52 = (bf16[1,2,4,256,576]{4,3,2,1,0:T(8,128)(2,1)}, bf16[2,4,256,576]{3,2,1,0:T(8,128)(2,1)S(1)}) fusion(bf16[1,4,256,576]{3,2,1,0:T(8,128)(2,1)} %bitcast.48, bf16[1,4,256,576]{3,2,1,0:T(8,128)(2,1)} %bitcast.49), kind=kLoop, calls=%fused_computation.93 | loop fusion | flops 1179648 | bytes 7077888 | tf_op jit(solution)/shard_map/stack | solution.py:51
  63.8 2.6 %copy.73 = bf16[2,4,256,576]{2,3,1,0:T(8,128)(2,1)} copy(bf16[2,4,256,576]{3,2,1,0:T(8,128)(2,1)S(1)} %get-tuple-element.8) | data formatting | bytes 4718592 | tf_op jit(solution)/shard_map/stack | solution.py:49
  66.3 2.0 collective-permute-start.1
  68.4 4.1 %all-to-all-start.3 = ((bf16[4,112,512]{2,1,0:T(8,128)(2,1)}), bf16[4,112,512]{2,1,0:T(8,128)(2,1)}, u32[]{:S(2)}, u32[]{:S(2)}) async-start(bf16[4,112,512]{2,1,0:T(8,128)(2,1)} %bitcast.57), calls=%async_computation.3 | async-start | bytes 917504 | tf_op jit(solution)/shard_map/all_to_all | solution.py:42
  75.9 3.1 %copy.74 = bf16[2,4,256,576]{3,2,1,0:T(8,128)(2,1)S(1)} copy(bf16[2,4,256,576]{2,3,1,0:T(8,128)(2,1)} %collective-permute-done.1) | data formatting | bytes 4718592 | tf_op jit(solution)/shard_map/ppermute | solution.py:50
  79.0 2.6 %pad_maximum_fusion = bf16[2,2,4,256,576]{4,3,2,1,0:T(8,128)(2,1)S(1)} fusion(bf16[1,2,4,256,576]{4,3,2,1,0:T(8,128)(2,1)S(1)} %bitcast.42, bf16[1,2,4,256,576]{4,3,2,1,0:T(8,128)(2,1)} %get-tuple-element.7), kind=kLoop, calls=%fused_computation.5 | loop fusion | flops 2359296 | bytes 9437184 | tf_op jit(solution)/shard_map/stack | solution.py:51
  81.6 4.1 %select_reduce_fusion = (f32[512]{0:T(512)S(1)}, f32[512,4096]{1,0:T(8,128)S(1)}) fusion(s32[4096]{0:T(1024)S(1)} %add_add_fusion, s32[512]{0:T(512)S(1)} %fusion.44, pred[4096]{0:T(1024)(128)(4,1)S(1)} %get-tuple-element.11, pred[4096]{0:T(1024)(128)(4,1)S(1)} %get-tuple-element.12, bf16[4096,576]{1,0:T(8,128)(2,1)S(1)} %bitcast.46, ...), kind=kOutput, calls=%fused_computation.1 | convolution fusion | flops 2427584000 | bytes 13725696 | tf_op jit(solution)/shard_map/dot_general | solution.py:89
  85.6 3.4 %fusion = f32[512]{0:T(512)S(1)} fusion(f32[512,4096]{1,0:T(8,128)S(1)} %get-tuple-element.10, f32[512]{0:T(512)S(1)} %get-tuple-element.9, s32[4096]{0:T(1024)S(1)} %add_add_fusion, s32[512]{0:T(512)S(1)} %fusion.44, pred[4096]{0:T(1024)(128)(4,1)S(1)} %get-tuple-element.11, pred[4096]{0:T(1024)(128)(4,1)S(1)} %get-tuple-element.12), kind=kLoop, calls=%fused_computation.3 | loop fusion | flops 12582400 | bytes 8419328 | tf_op jit(solution)/shard_map/reduce_sum | solution.py:94
  89.1 2.5 %divide_convert_fusion = bf16[512,512]{1,0:T(8,128)(2,1)S(1)} fusion(bf16[4096,576]{1,0:T(8,128)(2,1)S(1)} %bitcast.47, f32[512,4096]{1,0:T(8,128)S(1)} %get-tuple-element.10, f32[512]{0:T(512)S(1)} %get-tuple-element.9, s32[4096]{0:T(1024)S(1)} %add_add_fusion, s32[512]{0:T(512)S(1)} %fusion.44, pred[4096]{0:T(1024)(128)(4,1)S(1)} %get-tuple-element.11, ...), kind=kOutput, calls=%fused_computation.20 | convolution fusion | flops 2160590848 | bytes 13137920 | tf_op jit(solution)/shard_map/dot_general | solution.py:95
  92.2 1.5 broadcast_in_dim.85
  93.8 7.4 %all-to-all-start.2 = ((bf16[16,128,512]{2,1,0:T(8,128)(2,1)}), bf16[16,128,512]{2,1,0:T(8,128)(2,1)S(1)}, u32[]{:S(2)}, u32[]{:S(2)}) async-start(bf16[16,128,512]{2,1,0:T(8,128)(2,1)} %broadcast_in_dim.85), calls=%async_computation.2 | async-start | bytes 4194304 | tf_op jit(solution)/shard_map/all_to_all | solution.py:15
  101.2 8.2 %collective-permute-start.2 = (bf16[112,4,512]{2,0,1:T(8,128)(2,1)}, bf16[112,4,512]{2,0,1:T(8,128)(2,1)S(1)}, u32[]{:S(2)}, u32[]{:S(2)}) collective-permute-start(bf16[112,4,512]{2,0,1:T(8,128)(2,1)} %bitcast.13), channel_id=1, source_target_pairs={{0,64},{64,0},{1,65},{65,1},{2,66},{66,2},{3,67},{67,3},{4,68},{68... | collective-permute-start | bytes 1376264 | tf_op jit(solution)/shard_map/ppermute | solution.py:48
  109.4 43.3 %collective-permute-done.2 = bf16[112,4,512]{2,0,1:T(8,128)(2,1)S(1)} collective-permute-done((bf16[112,4,512]{2,0,1:T(8,128)(2,1)}, bf16[112,4,512]{2,0,1:T(8,128)(2,1)S(1)}, u32[]{:S(2)}, u32[]{:S(2)}) %collective-permute-start.2) | collective-permute-done | bytes 458784 | tf_op jit(solution)/shard_map/ppermute | solution.py:48
  152.7 2.3 %maximum_select_fusion.2 = bf16[2,112,4,512]{3,1,2,0:T(8,128)(2,1)} fusion(bf16[1,112,4,512]{3,1,2,0:T(8,128)(2,1)S(1)} %bitcast.54, bf16[1,112,4,512]{3,1,2,0:T(8,128)(2,1)} %bitcast.17, pred[]{:T(512)S(6)} %eq.39), kind=kLoop, calls=%fused_computation.22 | loop fusion | flops 1376256 | bytes 1835009 | tf_op jit(solution)/shard_map/jit(_where)/select_n | solution.py:54
  155.0 2.1 collective-permute-start.3
  159.7 1.8 maximum_select_fusion
  161.5 1.4 copy.80
  162.9 1.8 copy.90
  164.7 2.0 copy.79
  169.6 1.9 collective-permute-start.4
  171.5 8.3 %collective-permute-done.4 = bf16[2,2,1,64,448]{4,3,2,1,0:T(8,128)(2,1)S(1)} collective-permute-done((bf16[2,2,1,64,448]{4,3,2,1,0:T(8,128)(2,1)S(1)}, bf16[2,2,1,64,448]{4,3,2,1,0:T(8,128)(2,1)S(1)}, u32[]{:S(2)}, u32[]{:S(2)}) %collective-permute-start.4) | collective-permute-done | bytes 229408 | tf_op jit(solution)/shard_map/ppermute | solution.py:112
  179.9 1.9 collective-permute-start.5
  181.9 8.3 %collective-permute-done.5 = bf16[2,1,1,64,448]{4,3,2,1,0:T(8,128)(2,1)S(1)} collective-permute-done((bf16[2,1,1,64,448]{4,3,2,1,0:T(8,128)(2,1)S(1)}, bf16[2,1,1,64,448]{4,3,2,1,0:T(8,128)(2,1)S(1)}, u32[]{:S(2)}, u32[]{:S(2)}) %collective-permute-start.5) | collective-permute-done | bytes 114720 | tf_op jit(solution)/shard_map/ppermute | solution.py:112
  190.3 3.8 %collective-permute-start.6 = (bf16[1,1,1,64,448]{4,3,2,1,0:T(8,128)(2,1)S(1)}, bf16[1,1,1,64,448]{4,3,2,1,0:T(8,128)(2,1)S(1)}, u32[]{:S(2)}, u32[]{:S(2)}) collective-permute-start(bf16[1,1,1,64,448]{4,3,2,1,0:T(8,128)(2,1)S(1)} %constant_dynamic-slice_fusion.3), channel_id=1, source_target_pairs={{0,16},{4,20},{8,24},{12,28},{16,0},{20,4},{24,8},{28,12},{1,17},{... | collective-permute-start | bytes 172040 | tf_op jit(solution)/shard_map/ppermute | solution.py:112
  194.1 7.7 %collective-permute-done.6 = bf16[1,1,1,64,448]{4,3,2,1,0:T(8,128)(2,1)S(1)} collective-permute-done((bf16[1,1,1,64,448]{4,3,2,1,0:T(8,128)(2,1)S(1)}, bf16[1,1,1,64,448]{4,3,2,1,0:T(8,128)(2,1)S(1)}, u32[]{:S(2)}, u32[]{:S(2)}) %collective-permute-start.6) | collective-permute-done | bytes 57376 | tf_op jit(solution)/shard_map/ppermute | solution.py:112
  201.9 12.7 %all_to_all.25 = bf16[16,4,448]{2,1,0:T(4,128)(2,1)S(1)} all-to-all(bf16[16,4,448]{2,1,0:T(4,128)(2,1)S(1)} %reshape.219), channel_id=1, replica_groups=mesh['x'=4,'zh'=2,'core'=2,'zl'=8,'y'=4] {'x','y'}, dimensions={0} | all-to-all | bytes 114688 | tf_op jit(solution)/shard_map/all_to_all | solution.py:116
  (56 shorter events, 15.3 us)
Async XLA Ops:
  0.0 72.5 %copy-start = (bf16[4,128,512]{2,1,0:T(8,128)(2,1)S(1)}, bf16[4,128,512]{2,1,0:T(8,128)(2,1)}, u32[]{:S(2)}) copy-start(bf16[4,128,512]{2,1,0:T(8,128)(2,1)} %param.11) | copy-start | bytes 1572868
  3.1 29.2 %all-to-all-start = ((bf16[4,256,576]{1,2,0:T(8,128)(2,1)}), bf16[4,256,576]{1,2,0:T(8,128)(2,1)S(1)}, u32[]{:S(2)}, u32[]{:S(2)}) async-start(bf16[4,256,576]{1,2,0:T(8,128)(2,1)} %broadcast_in_dim.80), calls=%async_computation | async-start | bytes 2359296 | tf_op jit(solution)/shard_map/all_to_all | solution.py:15
  12.5 19.6 %collective-permute-start = (bf16[64,576]{0,1:T(8,128)(2,1)S(1)}, bf16[64,576]{0,1:T(8,128)(2,1)S(1)}, u32[]{:S(2)}, u32[]{:S(2)}) collective-permute-start(bf16[64,576]{0,1:T(8,128)(2,1)S(1)} %constant_dynamic-slice_fusion.2), channel_id=1, source_target_pairs={{0,92},{4,88},{8,84},{12,80},{16,76},{20,72},{24,68},{28,64},{64,2... | collective-permute-start | bytes 221192 | tf_op jit(solution)/shard_map/ppermute | solution.py:37
  33.5 25.5 %all-to-all-start.1 = ((bf16[16,64,576]{2,1,0:T(8,128)(2,1)}), bf16[16,64,576]{2,1,0:T(8,128)(2,1)S(1)}, u32[]{:S(2)}, u32[]{:S(2)}) async-start(bf16[16,64,576]{2,1,0:T(8,128)(2,1)} %broadcast_in_dim.81), calls=%async_computation.1 | async-start | bytes 2621440 | tf_op jit(solution)/shard_map/all_to_all | solution.py:15
  59.0 1.0 copy-start.1
  63.8 8.8 %copy-start.5 = (bf16[128,4,128]{2,1,0:T(4,128)(2,1)S(1)}, bf16[128,4,128]{2,1,0:T(4,128)(2,1)}, u32[]{:S(2)}) copy-start(bf16[128,4,128]{2,1,0:T(4,128)(2,1)} %param.9) | copy-start | bytes 393220
  66.3 7.8 %copy-start.6 = (bf16[128,4,64]{0,2,1:T(8,128)(2,1)S(1)}, bf16[128,4,64]{0,2,1:T(8,128)(2,1)}, u32[]{:S(2)}) copy-start(bf16[128,4,64]{0,2,1:T(8,128)(2,1)} %param.10) | copy-start | bytes 196612
  66.3 8.0 %copy-start.8 = (s32[16]{0:T(128)S(1)}, s32[16]{0:T(128)}, u32[]{:S(2)}) copy-start(s32[16]{0:T(128)} %param.16) | copy-start | bytes 196
  66.3 9.3 %copy-start.7 = (s32[16]{0:T(128)S(1)}, s32[16]{0:T(128)}, u32[]{:S(2)}) copy-start(s32[16]{0:T(128)} %param.17) | copy-start | bytes 196
  66.3 9.5 %collective-permute-start.1 = (bf16[2,4,256,576]{2,3,1,0:T(8,128)(2,1)}, bf16[2,4,256,576]{2,3,1,0:T(8,128)(2,1)}, u32[]{:S(2)}, u32[]{:S(2)}) collective-permute-start(bf16[2,4,256,576]{2,3,1,0:T(8,128)(2,1)} %copy.73), channel_id=1, source_target_pairs={{0,32},{32,0},{1,33},{33,1},{2,34},{34,2},{3,35},{35,3},{4,36},{36... | collective-permute-start | bytes 7077896 | tf_op jit(solution)/shard_map/ppermute | solution.py:50
  68.4 23.9 %all-to-all-start.3 = ((bf16[4,112,512]{2,1,0:T(8,128)(2,1)}), bf16[4,112,512]{2,1,0:T(8,128)(2,1)}, u32[]{:S(2)}, u32[]{:S(2)}) async-start(bf16[4,112,512]{2,1,0:T(8,128)(2,1)} %bitcast.57), calls=%async_computation.3 | async-start | bytes 917504 | tf_op jit(solution)/shard_map/all_to_all | solution.py:42
  79.0 2.6 %copy-start.4 = (bf16[512,512]{1,0:T(8,128)(2,1)S(1)}, bf16[512,512]{1,0:T(8,128)(2,1)}, u32[]{:S(2)}) copy-start(bf16[512,512]{1,0:T(8,128)(2,1)} %concatenate.26) | copy-start | bytes 1572868
  89.1 2.7 %copy-start.3 = (bf16[4,512,128]{2,1,0:T(8,128)(2,1)S(1)}, bf16[4,512,128]{2,1,0:T(8,128)(2,1)}, u32[]{:S(2)}) copy-start(bf16[4,512,128]{2,1,0:T(8,128)(2,1)} %param.12) | copy-start | bytes 1572868
  93.8 70.9 %all-to-all-start.2 = ((bf16[16,128,512]{2,1,0:T(8,128)(2,1)}), bf16[16,128,512]{2,1,0:T(8,128)(2,1)S(1)}, u32[]{:S(2)}, u32[]{:S(2)}) async-start(bf16[16,128,512]{2,1,0:T(8,128)(2,1)} %broadcast_in_dim.85), calls=%async_computation.2 | async-start | bytes 4194304 | tf_op jit(solution)/shard_map/all_to_all | solution.py:15
  101.2 51.5 %collective-permute-start.2 = (bf16[112,4,512]{2,0,1:T(8,128)(2,1)}, bf16[112,4,512]{2,0,1:T(8,128)(2,1)S(1)}, u32[]{:S(2)}, u32[]{:S(2)}) collective-permute-start(bf16[112,4,512]{2,0,1:T(8,128)(2,1)} %bitcast.13), channel_id=1, source_target_pairs={{0,64},{64,0},{1,65},{65,1},{2,66},{66,2},{3,67},{67,3},{4,68},{68... | collective-permute-start | bytes 1376264 | tf_op jit(solution)/shard_map/ppermute | solution.py:48
  155.0 4.7 %collective-permute-start.3 = (bf16[2,112,4,512]{3,1,2,0:T(8,128)(2,1)}, bf16[2,112,4,512]{3,1,2,0:T(8,128)(2,1)}, u32[]{:S(2)}, u32[]{:S(2)}) collective-permute-start(bf16[2,112,4,512]{3,1,2,0:T(8,128)(2,1)} %maximum_select_fusion.2), channel_id=1, source_target_pairs={{0,32},{32,0},{1,33},{33,1},{2,34},{34,2},{3,35},{35,3},{4,36},{36... | collective-permute-start | bytes 2752520 | tf_op jit(solution)/shard_map/ppermute | solution.py:55
  166.7 1.5 copy-start.2
  169.6 10.2 %collective-permute-start.4 = (bf16[2,2,1,64,448]{4,3,2,1,0:T(8,128)(2,1)S(1)}, bf16[2,2,1,64,448]{4,3,2,1,0:T(8,128)(2,1)S(1)}, u32[]{:S(2)}, u32[]{:S(2)}) collective-permute-start(bf16[2,2,1,64,448]{4,3,2,1,0:T(8,128)(2,1)S(1)} %constant_dynamic-slice_fusion.1), channel_id=1, source_target_pairs={{0,4},{4,0},{8,12},{12,8},{16,20},{20,16},{24,28},{28,24},{1,5},{5... | collective-permute-start | bytes 688136 | tf_op jit(solution)/shard_map/ppermute | solution.py:112
  179.9 10.3 %collective-permute-start.5 = (bf16[2,1,1,64,448]{4,3,2,1,0:T(8,128)(2,1)S(1)}, bf16[2,1,1,64,448]{4,3,2,1,0:T(8,128)(2,1)S(1)}, u32[]{:S(2)}, u32[]{:S(2)}) collective-permute-start(bf16[2,1,1,64,448]{4,3,2,1,0:T(8,128)(2,1)S(1)} %constant_dynamic-slice_fusion), channel_id=1, source_target_pairs={{0,8},{4,12},{8,0},{12,4},{16,24},{20,28},{24,16},{28,20},{1,9},{5... | collective-permute-start | bytes 344072 | tf_op jit(solution)/shard_map/ppermute | solution.py:112
  190.3 11.6 %collective-permute-start.6 = (bf16[1,1,1,64,448]{4,3,2,1,0:T(8,128)(2,1)S(1)}, bf16[1,1,1,64,448]{4,3,2,1,0:T(8,128)(2,1)S(1)}, u32[]{:S(2)}, u32[]{:S(2)}) collective-permute-start(bf16[1,1,1,64,448]{4,3,2,1,0:T(8,128)(2,1)S(1)} %constant_dynamic-slice_fusion.3), channel_id=1, source_target_pairs={{0,16},{4,20},{8,24},{12,28},{16,0},{20,4},{24,8},{28,12},{1,17},{... | collective-permute-start | bytes 172040 | tf_op jit(solution)/shard_map/ppermute | solution.py:112

commit v2 on v0

v2 whole, which is shorter than its diff:
```python
import functools

import jax
import jax.numpy as jnp
from jax import lax
from jax.experimental import pallas as pl
from jax.experimental.pallas import tpu as pltpu
from jax.sharding import Mesh
from jax.sharding import PartitionSpec as P


neg_large = -1e30
f32 = jnp.float32
bf16 = jnp.bfloat16
swap = ((0, 1), (1, 0))
VMEM = pl.BlockSpec(memory_space=pltpu.VMEM)
SMEM = pl.BlockSpec(memory_space=pltpu.SMEM)


def spread(value, axes):
    count = lax.axis_size(axes)
    copies = jnp.broadcast_to(value[None], (count,) + value.shape)
    return lax.all_to_all(copies, axes, 0, 0, tiled=False)


def cost(flops, nbytes, trans=0):
    return pl.CostEstimate(flops=flops, bytes_accessed=nbytes, transcendentals=trans)


def pack_body(latent_width, cache_ref, new_ref, out_ref):
    rope = cache_ref.shape[1] - latent_width
    for copy in range(out_ref.shape[0]):
        out_ref[copy, :, :latent_width] = cache_ref[:, :latent_width]
        out_ref[copy, :, latent_width : 2 * latent_width] = new_ref[:, :latent_width]
        out_ref[copy, :, 2 * latent_width : 2 * latent_width + rope] = cache_ref[:, latent_width:]
        out_ref[copy, :, 2 * latent_width + rope :] = new_ref[:, latent_width:]


def pack(cache, new, latent_width, copies):
    rows = cache.shape[0]
    shape = (copies, rows, 2 * cache.shape[1])
    return pl.pallas_call(
        functools.partial(pack_body, latent_width),
        out_shape=jax.ShapeDtypeStruct(shape, bf16),
        in_specs=[VMEM, VMEM],
        out_specs=VMEM,
        cost_estimate=cost(0, 4 * shape[0] * shape[1] * shape[2]),
        name="pack",
    )(cache, new)


def attend_body(first, last, pieces, scale, *refs):
    refs = list(refs)
    ql_ref, qr_ref, limit_ref, where_ref = refs[:4]
    keys = refs[4 : 4 + pieces]
    refs = refs[4 + pieces :]
    if not first:
        m_in, l_in, acc_in = refs[:3]
        refs = refs[3:]
    if last:
        wuv_ref = refs[0]
        refs = refs[1:]
    heads, toks, width = ql_ref.shape
    part = keys[0].shape[0] * keys[0].shape[1]
    slots = lax.broadcasted_iota(jnp.int32, (toks, part), 1) % keys[0].shape[1]
    tok = lax.broadcasted_iota(jnp.int32, (toks, part), 0)
    nt = (((1,), (1,)), ((), ()))
    seen_cache = [slots < limit_ref[p : p + 1, :] for p in range(pieces)]
    seen_new = [where_ref[p : p + 1, :] + slots <= tok for p in range(pieces)]
    for h in range(heads):
        scores = []
        for p in range(pieces):
            rope = keys[p][:, :, 2 * width :].reshape(part, -1)
            for kind in range(2):
                lat = keys[p][:, :, kind * width : (kind + 1) * width].reshape(part, width)
                s = lax.dot_general(ql_ref[h], lat, nt, preferred_element_type=f32)
                s = s + lax.dot_general(qr_ref[kind, h], rope, nt, preferred_element_type=f32)
                seen = seen_new[p] if kind else seen_cache[p]
                scores.append(jnp.where(seen, s, neg_large))
        top = functools.reduce(jnp.maximum, scores)
        top = jnp.max(top, axis=1, keepdims=True)
        if first:
            m = top
            total = jnp.zeros((toks, 1), f32)
            acc = None
        else:
            m_old = m_in[h][:, :1]
            m = jnp.maximum(top, m_old)
            keep = jnp.exp2((m_old - m) * scale)
            total = l_in[h][:, :1] * keep
            acc = acc_in[h] * keep
        at = 0
        for p in range(pieces):
            for kind in range(2):
                lat = keys[p][:, :, kind * width : (kind + 1) * width].reshape(part, width)
                e = jnp.exp2((scores[at] - m) * scale)
                at += 1
                total = total + jnp.sum(e, axis=1, keepdims=True)
                d = jnp.dot(e.astype(bf16), lat, preferred_element_type=f32)
                acc = d if acc is None else acc + d
        if last:
            out = (acc / total).astype(bf16)
            wide = jnp.dot(out, wuv_ref[h], preferred_element_type=f32)
            refs[0][:, h * wide.shape[1] : (h + 1) * wide.shape[1]] = wide.astype(bf16)
        else:
            refs[0][h] = jnp.broadcast_to(m, (toks, 128))
            refs[1][h] = jnp.broadcast_to(total, (toks, 128))
            refs[2][h] = acc


def attend(ql, qr, limits, where, keys, scale, state=None, w_uv=None):
    heads, toks, width = ql.shape
    first, last = state is None, w_uv is not None
    args = [ql, qr, limits, where, *keys]
    if not first:
        args += list(state)
    if last:
        args.append(w_uv)
        out_shape = jax.ShapeDtypeStruct((toks, heads * w_uv.shape[2]), bf16)
    else:
        out_shape = (
            jax.ShapeDtypeStruct((heads, toks, 128), f32),
            jax.ShapeDtypeStruct((heads, toks, 128), f32),
            jax.ShapeDtypeStruct((heads, toks, width), f32),
        )
    count = 2 * len(keys) * keys[0].shape[0] * keys[0].shape[1]
    rows = heads * toks
    return pl.pallas_call(
        functools.partial(attend_body, first, last, len(keys), scale),
        out_shape=out_shape,
        in_specs=[VMEM] * len(args),
        out_specs=VMEM if last else (VMEM,) * 3,
        cost_estimate=cost(4 * rows * count * width, 4 * count * width, rows * count),
        name="attend",
    )(*args)


def join_body(flag_ref, near_ref, far_ref, near_other_ref, far_other_ref, out_ref):
    groups, cols = near_ref.shape[0], near_ref.shape[1]
    zh, core, y = flag_ref[0], flag_ref[1], flag_ref[2]
    for ref, a, b in (
        (near_ref, 0, 0),
        (far_ref, 1, 0),
        (near_other_ref, 0, 1),
        (far_other_ref, 1, 1),
    ):
        slot = lax.bitwise_xor(zh, a) * 2 + lax.bitwise_xor(core, b)
        rows = pl.ds(pl.multiple_of(slot * cols, 16), cols)
        for k in range(groups):
            out_ref[lax.rem(y + groups - k, groups), rows, :] = ref[k]


def join(flags, pieces):
    groups, cols, depth = pieces[0].shape
    return pl.pallas_call(
        join_body,
        out_shape=jax.ShapeDtypeStruct((groups, 4 * cols, depth), bf16),
        in_specs=[SMEM] + [VMEM] * 4,
        out_specs=VMEM,
        cost_estimate=cost(0, 16 * groups * cols * depth),
        name="join",
    )(flags, *pieces)


def project_body(zb_size, ho_ref, w_ref, out_ref):
    nt = (((1,), (1,)), ((), ()))
    acc = None
    for y in range(ho_ref.shape[0]):
        d = lax.dot_general(ho_ref[y], w_ref[y], nt, preferred_element_type=f32)
        acc = d if acc is None else acc + d
    acc = acc.astype(bf16)
    rows = out_ref.shape[3]
    for za in range(out_ref.shape[1]):
        for zb in range(zb_size):
            at = (za * zb_size + zb) * rows
            out_ref[zb, za, 0] = acc[at : at + rows]


def project(ho, w, x_size, za_size, zb_size):
    members, toks, depth = ho.shape
    y_size, cols = w.shape[0], w.shape[1]
    rows = toks // (za_size * zb_size)
    return pl.pallas_call(
        functools.partial(project_body, zb_size),
        grid=(x_size,),
        out_shape=jax.ShapeDtypeStruct((zb_size, za_size, x_size, rows, cols), bf16),
        in_specs=[
            pl.BlockSpec((y_size, toks, depth), lambda x: (x, 0, 0)),
            pl.BlockSpec((y_size, cols, depth), lambda x: (0, 0, 0)),
        ],
        out_specs=pl.BlockSpec((zb_size, za_size, 1, rows, cols), lambda x: (0, 0, x, 0, 0)),
        cost_estimate=cost(2 * members * toks * depth * cols, 2 * members * toks * depth),
        name="project",
    )(ho, w)


def layer(q_nope, q_rope, w_uk, w_uv, w_o, cache_kv, new_kv, block_order, cache_lengths):
    tok_rows, _, nope_width = q_nope.shape
    latent_width = w_uk.shape[2]
    x_size, zh_size, core_size, za_size, zb_size, y_size = (
        lax.axis_size(a) for a in ("x", "zh", "core", "za", "zb", "y")
    )
    x_at, zh_at, core_at, y_at = (lax.axis_index(a) for a in ("x", "zh", "core", "y"))
    scale = float(nope_width + q_rope.shape[2]) ** (-0.5) * 1.4426950408889634

    quarter_rows = tok_rows // y_size
    start = y_at * quarter_rows
    quarter = pack(
        lax.dynamic_slice_in_dim(cache_kv, start, quarter_rows, 0),
        lax.dynamic_slice_in_dim(new_kv, start, quarter_rows, 0),
        latent_width,
        1,
    )[0]
    line = zh_size * za_size * zb_size
    mirror = [(i, line - 1 - i) for i in range(line)]
    far_quarter = lax.ppermute(quarter, ("zh", "za", "zb"), mirror)

    value_rows, col_count = w_o.shape
    cols = col_count // y_size
    w_t = w_o.T.reshape(y_size, cols, value_rows)
    parts = [lax.dynamic_index_in_dim(w_t, y_at, 0)]
    for k in range(1, y_size):
        part = lax.dynamic_index_in_dim(w_t, (y_at + k) % y_size, 0)
        parts.append(lax.ppermute(part, "y", [(i, (i + k) % y_size) for i in range(y_size)]))
    w_t = jnp.concatenate(parts, axis=0)
    copies = pack(cache_kv, new_kv, latent_width, x_size)
    near = lax.all_to_all(copies, "x", 0, 0, tiled=False)
    far = spread(far_quarter, ("x", "y"))
    far = far.reshape(x_size, tok_rows, -1)
    w_far = lax.ppermute(w_t, "zh", swap)
    near_other = lax.ppermute(near, "core", swap)
    far_other = lax.ppermute(far, "core", swap)
    w_other = lax.ppermute(w_t, "core", swap)
    w_far_other = lax.ppermute(w_far, "core", swap)

    ql = jnp.einsum("thn,hnc->htc", q_nope, w_uk, preferred_element_type=f32).astype(bf16)
    rope = jnp.transpose(q_rope, (1, 0, 2))
    blank = jnp.zeros_like(rope)
    qr = jnp.stack([jnp.concatenate([rope, blank], axis=2), jnp.concatenate([blank, rope], axis=2)])
    ctx_count = x_size * zh_size * core_size
    shard_ids = jnp.arange(ctx_count, dtype=jnp.int32)
    own_ctx = (x_at * zh_size + zh_at) * core_size + core_at
    own_block = jnp.sum(jnp.where(shard_ids == own_ctx, block_order, 0))

    def of_piece(zh_flip, core_flip):
        column = jnp.arange(x_size * tok_rows, dtype=jnp.int32) // tok_rows
        owner = (column * zh_size + (zh_at ^ zh_flip)) * core_size + (core_at ^ core_flip)
        hit = owner[:, None] == shard_ids[None, :]
        limit = jnp.sum(jnp.where(hit, cache_lengths[None, :], 0), axis=1)
        block = jnp.sum(jnp.where(hit, block_order[None, :], 0), axis=1)
        return limit, (block - own_block) * tok_rows

    tables = [of_piece(a, b) for a in range(2) for b in range(2)]
    limits = jnp.stack([t[0] for t in tables])
    where = jnp.stack([t[1] for t in tables])

    state = attend(ql, qr, limits[:2], where[:2], (near, near_other), scale)
    state = attend(ql, qr, limits[2:3], where[2:3], (far,), scale, state)
    head_out = attend(ql, qr, limits[3:], where[3:], (far_other,), scale, state, w_uv)

    gathered = spread(head_out, ("x", "y"))
    flags = jnp.stack([zh_at, core_at, y_at]).astype(jnp.int32)
    w_all = join(flags, (w_t, w_far, w_other, w_far_other))
    partial = project(gathered, w_all, x_size, za_size, zb_size)

    rows_out = tok_rows // (za_size * zb_size * y_size)
    width = partial.shape[-1]
    partial = partial.reshape(zb_size, -1, width)
    got = lax.all_to_all(partial, "zb", 0, 0, tiled=False)
    partial = jnp.sum(got.astype(f32), axis=0).astype(bf16)
    partial = partial.reshape(za_size * x_size * y_size, rows_out, width)
    got = lax.all_to_all(partial, ("za", "x", "y"), 0, 0, tiled=False)
    got = got.reshape(za_size, x_size, y_size, rows_out, zh_size * core_size, cols)
    mixed = jnp.sum(got.astype(f32), axis=0).astype(bf16)
    mixed = jnp.transpose(mixed, (2, 0, 3, 1, 4))
    return mixed.reshape(rows_out, -1)


def solution(mesh):
    axes = ("x", "zh", "core", "za", "zb", "y")
    fine = Mesh(mesh.devices.reshape(4, 2, 2, 2, 4, 4), axes)
    ctx, head = axes[:3], axes[3:]
    in_specs = (
        P(ctx, head, None),
        P(ctx, head, None),
        P(head, None, None),
        P(head, None, None),
        P(head, ctx),
        P(ctx, None),
        P(ctx, None),
        P(),
        P(),
    )
    out_specs = P(axes, None)
    return jax.shard_map(layer, mesh=fine, in_specs=in_specs, out_specs=out_specs, check_vma=False)
```

time: 769 us -> 238 us (0.31)
  waiting for transfers between devices: 724 us -> 82.5 us
  starting transfers between devices: 0.08 us -> 56.4 us
  blocking collectives: 0 us -> 38.5 us
  Pallas kernels: 0 us -> 33.8 us
  matrix products: 17.7 us -> 1.09 us
  between operations: 14.6 us -> 0.24 us
  local copies, waits for them, and re-layouts: 4.47 us -> 15.4 us
    unnamed x4 -> x0, waiting for transfers between devices: 451 us -> none
    all_gather x2 -> x0, waiting for transfers between devices: 273 us -> none  [the longest x1 146 us: on_device(): lax.all_gather(w_o, 'ctx', axis=1, tiled=True)]
    ppermute x0 -> x9, waiting for transfers between devices: none -> 71.6 us  [the longest x1 43 us: layer(): w_far = lax.ppermute(w_t, 'zh', swap)]
    all_to_all x0 -> x2, blocking collectives: none -> 38.5 us  [the longest x1 22.5 us: layer(): got = lax.all_to_all(partial, ('za', 'x', 'y'), 0, 0, tiled=False)]
    pallas_call x0 -> x7, Pallas kernels: none -> 33.8 us  [the longest x3 21.9 us: attend(): pl.pallas_call(functools.partial(attend_body, first, last, len(keys), sca...]
    ppermute x0 -> x9, starting transfers between devices: none -> 33.1 us  [the longest x3 11.3 us: layer(): lax.ppermute(part, 'y', [(i, (i + k) % y_size) for i in range(y_size)])]
    all_to_all x0 -> x3, starting transfers between devices: none -> 23.2 us  [the longest x2 13.9 us: spread(): return lax.all_to_all(copies, axes, 0, 0, tiled=False)]
    dot_general x5 -> x1, matrix products: 17.7 us -> 1.09 us  [layer(): jnp.einsum('thn,hnc->htc', q_nope, w_uk, preferred_element_type=f32)]
  transfers between devices with their start and end apart: 3 -> 12, of which waited for: 3 -> 7; matrix products, arithmetic and copies ran while one was open for 3% -> 4% of each run, Pallas kernels for 0% -> 8%
where the time goes in v2:
time: 238 us; the launch traced here: 236 us
  waiting for transfers between devices  82.5 us (35%)
  starting transfers between devices  56.4 us (24%)
  blocking collectives  38.5 us (16%)
  Pallas kernels  33.8 us (14%)
  local copies, waits for them, and re-layouts  15.4 us (6%)
  other arithmetic  7.87 us (3%)
    ppermute x1, waiting for transfers between devices, layer(): w_far = lax.ppermute(w_t, 'zh', swap)  43 us
    all_to_all x1, blocking collectives, layer(): got = lax.all_to_all(partial, ('za', 'x', 'y'), 0, 0, tiled=False)  22.5 us
    pallas_call x3, Pallas kernels, attend(): pl.pallas_call(functools.partial(attend_body, first, last, len(keys), sca...  21.9 us
    ppermute x3, waiting for transfers between devices, layer(): lax.ppermute(part, 'y', [(i, (i + k) % y_size) for i in range(y_size)])  21.4 us
    all_to_all x1, blocking collectives, layer(): got = lax.all_to_all(partial, 'zb', 0, 0, tiled=False)  16 us
    all_to_all x2, starting transfers between devices, spread(): return lax.all_to_all(copies, axes, 0, 0, tiled=False)  13.9 us
    ppermute x3, starting transfers between devices, layer(): lax.ppermute(part, 'y', [(i, (i + k) % y_size) for i in range(y_size)])  11.3 us
    all_to_all x2, waiting for transfers between devices, spread(): return lax.all_to_all(copies, axes, 0, 0, tiled=False)  10.9 us
  transfers between devices with their start and end apart: 12, of which 7 were waited for; matrix products, arithmetic and copies ran while one was open for 4% of the time, Pallas kernels for 8%

profile of v2, /device:TPU:6, one launch (start us, length us, event | category | flops | bytes accessed | tf_op | source)
XLA Modules:
  0.0 235.9 jit_solution(4849629582006855815)
XLA Ops:
  0.0 1.8 copy.48.cache_ref
  1.8 1.7 copy.49.new_ref
  3.5 2.2 pack.3
  5.6 9.3 %all-to-all-start.1 = ((bf16[4,128,1152]{2,1,0:T(8,128)(2,1)}), bf16[4,128,1152]{2,1,0:T(8,128)(2,1)S(1)}, u32[]{:S(2)}, u32[]{:S(2)}) async-start(bf16[4,128,1152]{2,1,0:T(8,128)(2,1)} %pack.3), calls=%async_computation.1 | async-start | bytes 2359296 | tf_op jit(solution)/shard_map/all_to_all | solution.py:227
  15.0 1.4 constant_dynamic-slice_fusion.4
  16.4 1.5 pack.2
  17.9 6.8 %collective-permute-start = (bf16[32,1152]{1,0:T(8,128)(2,1)}, bf16[32,1152]{1,0:T(8,128)(2,1)S(1)}, u32[]{:S(2)}, u32[]{:S(2)}) collective-permute-start(bf16[32,1152]{1,0:T(8,128)(2,1)} %bitcast.30), channel_id=1, source_target_pairs={{0,92},{4,88},{8,84},{12,80},{16,76},{20,72},{24,68},{28,64},{64,2... | collective-permute-start | bytes 221192 | tf_op jit(solution)/shard_map/ppermute | solution.py:216
  24.8 6.6 %collective-permute-done = bf16[32,1152]{1,0:T(8,128)(2,1)S(1)} collective-permute-done((bf16[32,1152]{1,0:T(8,128)(2,1)}, bf16[32,1152]{1,0:T(8,128)(2,1)S(1)}, u32[]{:S(2)}, u32[]{:S(2)}) %collective-permute-start) | collective-permute-done | bytes 73760 | tf_op jit(solution)/shard_map/ppermute | solution.py:216
  32.6 7.6 %all-to-all-start = ((bf16[16,32,1152]{2,1,0:T(8,128)(2,1)}), bf16[16,32,1152]{2,1,0:T(8,128)(2,1)S(1)}, u32[]{:S(2)}, u32[]{:S(2)}) async-start(bf16[16,32,1152]{2,1,0:T(8,128)(2,1)} %broadcast_in_dim.79), calls=%async_computation | async-start | bytes 2359296 | tf_op jit(solution)/shard_map/all_to_all | solution.py:23
  42.3 1.9 collective-permute-start.2
  45.7 10.9 %all-to-all-done = bf16[16,32,1152]{2,1,0:T(8,128)(2,1)S(1)} async-done(((bf16[16,32,1152]{2,1,0:T(8,128)(2,1)}), bf16[16,32,1152]{2,1,0:T(8,128)(2,1)S(1)}, u32[]{:S(2)}, u32[]{:S(2)}) %all-to-all-start) | async-done | bytes 1179680 | tf_op jit(solution)/shard_map/all_to_all | solution.py:23
  57.7 1.9 collective-permute-start.1
  64.4 8.3 %attend.3 = (f32[4,128,128]{2,1,0:T(8,128)}, f32[4,128,128]{2,1,0:T(8,128)}, f32[4,128,512]{2,1,0:T(8,128)}) custom-call(bf16[4,128,512]{2,1,0:T(8,128)(2,1)} %convolution_convert_fusion.refs_0_, bf16[2,4,128,128]{3,2,1,0:T(8,128)(2,1)} %pad_maximum_fusion.1.refs_1_, s32[2,512]{1,0:T(2,128)} %pad_add_fusion.refs_2_, s32[2,512]{1,0:T(2,128)} %pad_add_fusion.1.refs_3_, ...), custom_call_target="tpu_custom_call" | custom-call | flops 2147483648 | bytes 4194304 | tf_op jit(solution)/shard_map/attend/pallas_call | solution.py:128
  72.8 6.7 %attend.4 = (f32[4,128,128]{2,1,0:T(8,128)}, f32[4,128,128]{2,1,0:T(8,128)}, f32[4,128,512]{2,1,0:T(8,128)}) custom-call(bf16[4,128,512]{2,1,0:T(8,128)(2,1)} %convolution_convert_fusion.refs_0_, bf16[2,4,128,128]{3,2,1,0:T(8,128)(2,1)} %pad_maximum_fusion.1.refs_1_, s32[1,512]{1,0:T(1,128)} %bitcast.37, s32[1,512]{1,0:T(1,128)} %bitcast.38, ...), custom_call_target="tpu_custom_call" | custom-call | flops 1073741824 | bytes 2097152 | tf_op jit(solution)/shard_map/attend/pallas_call | solution.py:128
  80.5 6.9 %attend.5 = bf16[128,512]{1,0:T(8,128)(2,1)} custom-call(bf16[4,128,512]{2,1,0:T(8,128)(2,1)} %convolution_convert_fusion.refs_0_, bf16[2,4,128,128]{3,2,1,0:T(8,128)(2,1)} %pad_maximum_fusion.1.refs_1_, s32[1,512]{1,0:T(1,128)} %bitcast.31, s32[1,512]{1,0:T(1,128)} %bitcast.32, bf16[4,128,1152]{2,1,0:T(8,128)(2,1)} %copy-done.3, ...), custom_call_target="tpu_custom_call" | custom-call | flops 1073741824 | bytes 2097152 | tf_op jit(solution)/shard_map/attend/pallas_call | solution.py:128
  87.3 2.4 %broadcast_in_dim.80 = bf16[16,128,512]{2,1,0:T(8,128)(2,1)} broadcast(bf16[128,512]{1,0:T(8,128)(2,1)} %attend.5), dimensions={1,2} | broadcast | bytes 2228224 | tf_op jit(solution)/shard_map/broadcast_in_dim | solution.py:22
  89.8 6.3 %all-to-all-start.2 = ((bf16[16,128,512]{2,1,0:T(8,128)(2,1)}), bf16[16,128,512]{2,1,0:T(8,128)(2,1)S(1)}, u32[]{:S(2)}, u32[]{:S(2)}) async-start(bf16[16,128,512]{2,1,0:T(8,128)(2,1)} %broadcast_in_dim.80), calls=%async_computation.2 | async-start | bytes 4194304 | tf_op jit(solution)/shard_map/all_to_all | solution.py:23
  96.1 3.4 %collective-permute-start.3 = (bf16[1,112,512]{2,1,0:T(8,128)(2,1)S(1)}, bf16[1,112,512]{2,1,0:T(8,128)(2,1)S(1)}, u32[]{:S(2)}, u32[]{:S(2)}) collective-permute-start(bf16[1,112,512]{2,1,0:T(8,128)(2,1)S(1)} %get-tuple-element.34), channel_id=1, source_target_pairs={{0,1},{1,2},{2,3},{3,0},{4,5},{5,6},{6,7},{7,4},{8,9},{9,10},{10,1... | collective-permute-start | bytes 344072 | tf_op jit(solution)/shard_map/ppermute | solution.py:224
  99.5 4.6 %collective-permute-start.4 = (bf16[1,112,512]{2,1,0:T(8,128)(2,1)S(1)}, bf16[1,112,512]{2,1,0:T(8,128)(2,1)S(1)}, u32[]{:S(2)}, u32[]{:S(2)}) collective-permute-start(bf16[1,112,512]{2,1,0:T(8,128)(2,1)S(1)} %get-tuple-element.33), channel_id=1, source_target_pairs={{0,2},{1,3},{2,0},{3,1},{4,6},{5,7},{6,4},{7,5},{8,10},{9,11},{10,... | collective-permute-start | bytes 344072 | tf_op jit(solution)/shard_map/ppermute | solution.py:224
  104.1 3.4 %collective-permute-start.5 = (bf16[1,112,512]{2,1,0:T(8,128)(2,1)S(1)}, bf16[1,112,512]{2,1,0:T(8,128)(2,1)S(1)}, u32[]{:S(2)}, u32[]{:S(2)}) collective-permute-start(bf16[1,112,512]{2,1,0:T(8,128)(2,1)S(1)} %get-tuple-element.32), channel_id=1, source_target_pairs={{0,3},{1,0},{2,1},{3,2},{4,7},{5,4},{6,5},{7,6},{8,11},{9,8},{10,9... | collective-permute-start | bytes 344072 | tf_op jit(solution)/shard_map/ppermute | solution.py:224
  107.5 18.0 %collective-permute-done.3 = bf16[1,112,512]{2,1,0:T(8,128)(2,1)S(1)} collective-permute-done((bf16[1,112,512]{2,1,0:T(8,128)(2,1)S(1)}, bf16[1,112,512]{2,1,0:T(8,128)(2,1)S(1)}, u32[]{:S(2)}, u32[]{:S(2)}) %collective-permute-start.3) | collective-permute-done | bytes 114720 | tf_op jit(solution)/shard_map/ppermute | solution.py:224
  125.5 2.2 collective-permute-done.4
  129.0 7.3 %collective-permute-start.6 = (bf16[4,112,512]{2,1,0:T(8,128)(2,1)S(1)}, bf16[4,112,512]{2,1,0:T(8,128)(2,1)S(1)}, u32[]{:S(2)}, u32[]{:S(2)}) collective-permute-start(bf16[4,112,512]{2,1,0:T(8,128)(2,1)S(1)} %pad_maximum_fusion.near_ref), channel_id=1, source_target_pairs={{0,64},{64,0},{1,65},{65,1},{2,66},{66,2},{3,67},{67,3},{4,68},{68... | collective-permute-start | bytes 1376264 | tf_op jit(solution)/shard_map/ppermute | solution.py:230
  136.3 1.9 collective-permute-start.7
  138.2 43.0 %collective-permute-done.6.far_ref = bf16[4,112,512]{2,1,0:T(8,128)(2,1)S(1)} collective-permute-done((bf16[4,112,512]{2,1,0:T(8,128)(2,1)S(1)}, bf16[4,112,512]{2,1,0:T(8,128)(2,1)S(1)}, u32[]{:S(2)}, u32[]{:S(2)}) %collective-permute-start.6) | collective-permute-done | bytes 458784 | tf_op jit(solution)/shard_map/ppermute | solution.py:230
  181.2 1.9 collective-permute-start.8
  185.1 2.8 %join.1.w_ref = bf16[4,448,512]{2,1,0:T(8,128)(2,1)} custom-call(s32[3]{0:T(128)} %pad_add_fusion.2.flag_ref, bf16[4,112,512]{2,1,0:T(8,128)(2,1)} %copy-done.2, bf16[4,112,512]{2,1,0:T(8,128)(2,1)} %copy-done.7, bf16[4,112,512]{2,1,0:T(8,128)(2,1)} %copy-done.8, bf16[4,112,512]{2,1,0:T(8,128)(2,1)} %collective-permute-done.8.far_other_ref), custom_call_target="tpu_custom_call" | custom-call | bytes 3670016 | tf_op jit(solution)/shard_map/join/pallas_call | solution.py:155
  187.9 1.3 copy-done.1
  189.2 5.5 %project.1 = bf16[4,2,4,16,448]{4,3,2,1,0:T(8,128)(2,1)} custom-call(bf16[16,128,512]{2,1,0:T(8,128)(2,1)} %copy-done.1, bf16[4,448,512]{2,1,0:T(8,128)(2,1)} %join.1.w_ref), custom_call_target="tpu_custom_call" | custom-call | flops 939524096 | bytes 2097152 | tf_op jit(solution)/shard_map/project/pallas_call | solution.py:183
  194.7 1.3 copy.52
  196.0 16.0 %all_to_all.25 = bf16[4,128,448]{1,2,0:T(8,128)(2,1)S(1)} all-to-all(bf16[4,128,448]{1,2,0:T(8,128)(2,1)S(1)} %copy.52), channel_id=1, replica_groups=mesh['x'=4,'zh'=2,'core'=2,'za'=2,'zb'=4,'y'=4] {'zb'}, dimensions={0} | all-to-all | bytes 917504 | tf_op jit(solution)/shard_map/all_to_all | solution.py:269
  212.3 22.5 %all_to_all.26 = bf16[32,4,448]{2,1,0:T(4,128)(2,1)S(1)} all-to-all(bf16[32,4,448]{2,1,0:T(4,128)(2,1)S(1)} %reshape.109), channel_id=1, replica_groups=mesh['x'=4,'zh'=2,'core'=2,'za'=2,'zb'=4,'y'=4] {'za','x','y'}, dimensions={0} | all-to-all | bytes 229376 | tf_op jit(solution)/shard_map/all_to_all | solution.py:272
  (57 shorter events, 16.2 us)
Async XLA Ops:
  0.0 63.3 %copy-start = (bf16[4,128,512]{2,1,0:T(8,128)(2,1)S(1)}, bf16[4,128,512]{2,1,0:T(8,128)(2,1)}, u32[]{:S(2)}) copy-start(bf16[4,128,512]{2,1,0:T(8,128)(2,1)} %param.11) | copy-start | bytes 1572868
  5.6 25.7 %all-to-all-start.1 = ((bf16[4,128,1152]{2,1,0:T(8,128)(2,1)}), bf16[4,128,1152]{2,1,0:T(8,128)(2,1)S(1)}, u32[]{:S(2)}, u32[]{:S(2)}) async-start(bf16[4,128,1152]{2,1,0:T(8,128)(2,1)} %pack.3), calls=%async_computation.1 | async-start | bytes 2359296 | tf_op jit(solution)/shard_map/all_to_all | solution.py:227
  17.9 13.5 %collective-permute-start = (bf16[32,1152]{1,0:T(8,128)(2,1)}, bf16[32,1152]{1,0:T(8,128)(2,1)S(1)}, u32[]{:S(2)}, u32[]{:S(2)}) collective-permute-start(bf16[32,1152]{1,0:T(8,128)(2,1)} %bitcast.30), channel_id=1, source_target_pairs={{0,92},{4,88},{8,84},{12,80},{16,76},{20,72},{24,68},{28,64},{64,2... | collective-permute-start | bytes 221192 | tf_op jit(solution)/shard_map/ppermute | solution.py:216
  31.4 10.9 %copy-start.4 = (bf16[4,128,1152]{2,1,0:T(8,128)(2,1)}, bf16[4,128,1152]{2,1,0:T(8,128)(2,1)S(1)}, u32[]{:S(2)}) copy-start(bf16[4,128,1152]{2,1,0:T(8,128)(2,1)S(1)} %all-to-all-done.1.refs_4_) | copy-start | bytes 3538948
  32.6 7.6 %copy-start.11 = (s32[16]{0:T(128)S(1)}, s32[16]{0:T(128)}, u32[]{:S(2)}) copy-start(s32[16]{0:T(128)} %param.16) | copy-start | bytes 196
  32.6 8.3 %copy-start.12 = (s32[16]{0:T(128)S(1)}, s32[16]{0:T(128)}, u32[]{:S(2)}) copy-start(s32[16]{0:T(128)} %param.17) | copy-start | bytes 196
  32.6 12.3 %copy-start.10 = (bf16[128,4,64]{0,2,1:T(8,128)(2,1)S(1)}, bf16[128,4,64]{0,2,1:T(8,128)(2,1)}, u32[]{:S(2)}) copy-start(bf16[128,4,64]{0,2,1:T(8,128)(2,1)} %param.10) | copy-start | bytes 196612
  32.6 24.0 %all-to-all-start = ((bf16[16,32,1152]{2,1,0:T(8,128)(2,1)}), bf16[16,32,1152]{2,1,0:T(8,128)(2,1)S(1)}, u32[]{:S(2)}, u32[]{:S(2)}) async-start(bf16[16,32,1152]{2,1,0:T(8,128)(2,1)} %broadcast_in_dim.79), calls=%async_computation | async-start | bytes 2359296 | tf_op jit(solution)/shard_map/all_to_all | solution.py:23
  40.2 23.1 %copy-start.9 = (bf16[128,4,128]{2,1,0:T(4,128)(2,1)S(1)}, bf16[128,4,128]{2,1,0:T(4,128)(2,1)}, u32[]{:S(2)}) copy-start(bf16[128,4,128]{2,1,0:T(4,128)(2,1)} %param.9) | copy-start | bytes 393220
  42.3 22.1 %collective-permute-start.2 = (bf16[4,128,1152]{2,1,0:T(8,128)(2,1)S(1)}, bf16[4,128,1152]{2,1,0:T(8,128)(2,1)}, u32[]{:S(2)}, u32[]{:S(2)}) collective-permute-start(bf16[4,128,1152]{2,1,0:T(8,128)(2,1)S(1)} %all-to-all-done.1.refs_4_), channel_id=1, source_target_pairs={{0,32},{32,0},{1,33},{33,1},{2,34},{34,2},{3,35},{35,3},{4,36},{36... | collective-permute-start | bytes 3538952 | tf_op jit(solution)/shard_map/ppermute | solution.py:231
  56.6 1.0 copy-start.5
  57.7 21.8 %collective-permute-start.1 = (bf16[4,128,1152]{2,1,0:T(8,128)(2,1)}, bf16[4,128,1152]{2,1,0:T(8,128)(2,1)S(1)}, u32[]{:S(2)}, u32[]{:S(2)}) collective-permute-start(bf16[4,128,1152]{2,1,0:T(8,128)(2,1)} %bitcast.25), channel_id=1, source_target_pairs={{0,32},{32,0},{1,33},{33,1},{2,34},{34,2},{3,35},{35,3},{4,36},{36... | collective-permute-start | bytes 3538952 | tf_op jit(solution)/shard_map/ppermute | solution.py:232
  79.4 1.0 copy-start.3
  89.8 6.3 %copy-start.6 = (bf16[512,448]{0,1:T(8,128)(2,1)S(1)}, bf16[512,448]{0,1:T(8,128)(2,1)}, u32[]{:S(2)}) copy-start(bf16[512,448]{0,1:T(8,128)(2,1)} %param.13) | copy-start | bytes 1376260
  89.8 98.1 %all-to-all-start.2 = ((bf16[16,128,512]{2,1,0:T(8,128)(2,1)}), bf16[16,128,512]{2,1,0:T(8,128)(2,1)S(1)}, u32[]{:S(2)}, u32[]{:S(2)}) async-start(bf16[16,128,512]{2,1,0:T(8,128)(2,1)} %broadcast_in_dim.80), calls=%async_computation.2 | async-start | bytes 4194304 | tf_op jit(solution)/shard_map/all_to_all | solution.py:23
  96.1 29.4 %collective-permute-start.3 = (bf16[1,112,512]{2,1,0:T(8,128)(2,1)S(1)}, bf16[1,112,512]{2,1,0:T(8,128)(2,1)S(1)}, u32[]{:S(2)}, u32[]{:S(2)}) collective-permute-start(bf16[1,112,512]{2,1,0:T(8,128)(2,1)S(1)} %get-tuple-element.34), channel_id=1, source_target_pairs={{0,1},{1,2},{2,3},{3,0},{4,5},{5,6},{6,7},{7,4},{8,9},{9,10},{10,1... | collective-permute-start | bytes 344072 | tf_op jit(solution)/shard_map/ppermute | solution.py:224
  99.5 28.2 %collective-permute-start.4 = (bf16[1,112,512]{2,1,0:T(8,128)(2,1)S(1)}, bf16[1,112,512]{2,1,0:T(8,128)(2,1)S(1)}, u32[]{:S(2)}, u32[]{:S(2)}) collective-permute-start(bf16[1,112,512]{2,1,0:T(8,128)(2,1)S(1)} %get-tuple-element.33), channel_id=1, source_target_pairs={{0,2},{1,3},{2,0},{3,1},{4,6},{5,7},{6,4},{7,5},{8,10},{9,11},{10,... | collective-permute-start | bytes 344072 | tf_op jit(solution)/shard_map/ppermute | solution.py:224
  104.1 24.8 %collective-permute-start.5 = (bf16[1,112,512]{2,1,0:T(8,128)(2,1)S(1)}, bf16[1,112,512]{2,1,0:T(8,128)(2,1)S(1)}, u32[]{:S(2)}, u32[]{:S(2)}) collective-permute-start(bf16[1,112,512]{2,1,0:T(8,128)(2,1)S(1)} %get-tuple-element.32), channel_id=1, source_target_pairs={{0,3},{1,0},{2,1},{3,2},{4,7},{5,4},{6,5},{7,6},{8,11},{9,8},{10,9... | collective-permute-start | bytes 344072 | tf_op jit(solution)/shard_map/ppermute | solution.py:224
  129.0 56.1 %copy-start.2 = (bf16[4,112,512]{2,1,0:T(8,128)(2,1)}, bf16[4,112,512]{2,1,0:T(8,128)(2,1)S(1)}, u32[]{:S(2)}) copy-start(bf16[4,112,512]{2,1,0:T(8,128)(2,1)S(1)} %pad_maximum_fusion.near_ref) | copy-start | bytes 1376260
  129.0 52.3 %collective-permute-start.6 = (bf16[4,112,512]{2,1,0:T(8,128)(2,1)S(1)}, bf16[4,112,512]{2,1,0:T(8,128)(2,1)S(1)}, u32[]{:S(2)}, u32[]{:S(2)}) collective-permute-start(bf16[4,112,512]{2,1,0:T(8,128)(2,1)S(1)} %pad_maximum_fusion.near_ref), channel_id=1, source_target_pairs={{0,64},{64,0},{1,65},{65,1},{2,66},{66,2},{3,67},{67,3},{4,68},{68... | collective-permute-start | bytes 1376264 | tf_op jit(solution)/shard_map/ppermute | solution.py:230
  136.3 47.5 %collective-permute-start.7 = (bf16[4,112,512]{2,1,0:T(8,128)(2,1)S(1)}, bf16[4,112,512]{2,1,0:T(8,128)(2,1)S(1)}, u32[]{:S(2)}, u32[]{:S(2)}) collective-permute-start(bf16[4,112,512]{2,1,0:T(8,128)(2,1)S(1)} %pad_maximum_fusion.near_ref), channel_id=1, source_target_pairs={{0,32},{32,0},{1,33},{33,1},{2,34},{34,2},{3,35},{35,3},{4,36},{36... | collective-permute-start | bytes 1376264 | tf_op jit(solution)/shard_map/ppermute | solution.py:233
  181.2 3.8 %copy-start.7 = (bf16[4,112,512]{2,1,0:T(8,128)(2,1)}, bf16[4,112,512]{2,1,0:T(8,128)(2,1)S(1)}, u32[]{:S(2)}) copy-start(bf16[4,112,512]{2,1,0:T(8,128)(2,1)S(1)} %collective-permute-done.6.far_ref) | copy-start | bytes 1376260
  181.2 3.8 %collective-permute-start.8 = (bf16[4,112,512]{2,1,0:T(8,128)(2,1)S(1)}, bf16[4,112,512]{2,1,0:T(8,128)(2,1)}, u32[]{:S(2)}, u32[]{:S(2)}) collective-permute-start(bf16[4,112,512]{2,1,0:T(8,128)(2,1)S(1)} %collective-permute-done.6.far_ref), channel_id=1, source_target_pairs={{0,32},{32,0},{1,33},{33,1},{2,34},{34,2},{3,35},{35,3},{4,36},{36... | collective-permute-start | bytes 1376264 | tf_op jit(solution)/shard_map/ppermute | solution.py:234
  183.8 0.8 copy-start.8
  187.9 1.3 copy-start.1

commit v3 on v2

v3 whole, which is shorter than its diff:
```python
import functools

import jax
import jax.numpy as jnp
from jax import lax
from jax.experimental import pallas as pl
from jax.experimental.pallas import tpu as pltpu
from jax.sharding import Mesh
from jax.sharding import PartitionSpec as P


neg_large = -1e30
f32 = jnp.float32
bf16 = jnp.bfloat16
swap = ((0, 1), (1, 0))
VMEM = pl.BlockSpec(memory_space=pltpu.VMEM)
SMEM = pl.BlockSpec(memory_space=pltpu.SMEM)


def spread(value, axes):
    count = lax.axis_size(axes)
    copies = jnp.broadcast_to(value[None], (count,) + value.shape)
    return lax.all_to_all(copies, axes, 0, 0, tiled=False)


def grant(mib):
    return pltpu.CompilerParams(vmem_limit_bytes=mib << 20)


def cost(flops, nbytes, trans=0):
    return pl.CostEstimate(flops=flops, bytes_accessed=nbytes, transcendentals=trans)


def pack_body(latent_width, at_ref, cache_ref, new_ref, copies_ref, part_ref, row_ref):
    rope = cache_ref.shape[0] - latent_width
    row_ref[:latent_width] = cache_ref[:latent_width]
    row_ref[latent_width : 2 * latent_width] = new_ref[:latent_width]
    row_ref[2 * latent_width : 2 * latent_width + rope] = cache_ref[latent_width:]
    row_ref[2 * latent_width + rope :] = new_ref[latent_width:]
    rows = part_ref.shape[0]
    part_ref[...] = row_ref[pl.ds(pl.multiple_of(at_ref[0] * rows, 16), rows), :]
    for copy in range(copies_ref.shape[0]):
        copies_ref[copy] = row_ref[...]


def pack(cache, new, latent_width, copies, part, parts):
    width, slots = cache.shape
    depth = 2 * width
    return pl.pallas_call(
        functools.partial(pack_body, latent_width),
        out_shape=(
            jax.ShapeDtypeStruct((copies, depth, slots), bf16),
            jax.ShapeDtypeStruct((depth // parts, slots), bf16),
        ),
        in_specs=[SMEM, VMEM, VMEM],
        out_specs=(VMEM, VMEM),
        scratch_shapes=[pltpu.VMEM((depth, slots), bf16)],
        cost_estimate=cost(0, 2 * (copies + 2) * depth * slots),
        compiler_params=grant(6),
        name="pack",
    )(part.astype(jnp.int32).reshape(1), cache, new)


def attend_body(first, last, pieces, heads, scale, *refs):
    refs = list(refs)
    ql_ref, qr_ref, limit_ref, where_ref = refs[:4]
    keys = refs[4 : 4 + pieces]
    refs = refs[4 + pieces :]
    if not first:
        m_in, l_in, acc_in = refs[:3]
        refs = refs[3:]
    if last:
        wuv_ref = refs[0]
        refs = refs[1:]
    rows, width = ql_ref.shape
    toks = rows // heads
    shards, depth, slots = keys[0].shape
    part = shards * slots
    slot = lax.broadcasted_iota(jnp.int32, (1, part), 1) % slots
    tok = lax.broadcasted_iota(jnp.int32, (rows, 1), 0) % toks

    def features(p, start, stop):
        return jnp.concatenate([keys[p][s, start:stop, :] for s in range(shards)], axis=1)

    scores = []
    for p in range(pieces):
        rope = features(p, 2 * width, depth)
        for kind in range(2):
            lat = features(p, kind * width, (kind + 1) * width)
            s = jnp.dot(ql_ref[...], lat, preferred_element_type=f32)
            s = s + jnp.dot(qr_ref[kind], rope, preferred_element_type=f32)
            if kind:
                seen = where_ref[p : p + 1, :] + slot <= tok
            else:
                seen = jnp.broadcast_to(slot < limit_ref[p : p + 1, :], s.shape)
            scores.append(jnp.where(seen, s, neg_large))
    top = jnp.max(functools.reduce(jnp.maximum, scores), axis=1, keepdims=True)
    if first:
        m, total, acc = top, None, None
    else:
        m_old = m_in[:, :1]
        m = jnp.maximum(top, m_old)
        keep = jnp.exp2((m_old - m) * scale)
        total = l_in[:, :1] * keep
        acc = acc_in[...] * keep
    sums = None
    for at, s in enumerate(scores):
        p, kind = at // 2, at % 2
        lat = features(p, kind * width, (kind + 1) * width)
        e = jnp.exp2((s - m) * scale)
        sums = e if sums is None else sums + e
        d = lax.dot_general(e.astype(bf16), lat, (((1,), (1,)), ((), ())), preferred_element_type=f32)
        acc = d if acc is None else acc + d
    sums = jnp.sum(sums, axis=1, keepdims=True)
    total = sums if total is None else total + sums
    if last:
        out_ref, hold_ref, sem = refs
        out = (acc / total).astype(bf16)
        value = wuv_ref.shape[2]
        for h in range(heads):
            wide = jnp.dot(
                out[h * toks : (h + 1) * toks], wuv_ref[h], preferred_element_type=f32
            )
            hold_ref[:, h * value : (h + 1) * value] = wide.astype(bf16)
        sends = [
            pltpu.make_async_copy(hold_ref, out_ref.at[c], sem.at[c])
            for c in range(out_ref.shape[0])
        ]
        for send in sends:
            send.start()
        for send in sends:
            send.wait()
    else:
        refs[0][...] = jnp.broadcast_to(m, (rows, 128))
        refs[1][...] = jnp.broadcast_to(total, (rows, 128))
        refs[2][...] = acc


def attend(ql, qr, limits, where, keys, scale, heads, state=None, w_uv=None, copies=0):
    rows, width = ql.shape
    toks = rows // heads
    first, last = state is None, w_uv is not None
    args = [ql, qr, limits, where, *keys]
    scratch = []
    if not first:
        args += list(state)
    if last:
        args.append(w_uv)
        wide = heads * w_uv.shape[2]
        out_shape = jax.ShapeDtypeStruct((copies, toks, wide), bf16)
        scratch = [pltpu.VMEM((toks, wide), bf16), pltpu.SemaphoreType.DMA((copies,))]
    else:
        out_shape = (
            jax.ShapeDtypeStruct((rows, 128), f32),
            jax.ShapeDtypeStruct((rows, 128), f32),
            jax.ShapeDtypeStruct((rows, width), f32),
        )
    count = 2 * len(keys) * keys[0].shape[0] * keys[0].shape[2]
    return pl.pallas_call(
        functools.partial(attend_body, first, last, len(keys), heads, scale),
        out_shape=out_shape,
        in_specs=[VMEM] * len(args),
        out_specs=pl.BlockSpec(memory_space=pltpu.HBM) if last else (VMEM,) * 3,
        scratch_shapes=scratch,
        cost_estimate=cost(4 * rows * count * width, 4 * count * width, rows * count),
        compiler_params=grant(20),
        name="attend",
    )(*args)


def join_body(flag_ref, near_ref, far_ref, near_other_ref, far_other_ref, out_ref):
    groups, cols = near_ref.shape[0], near_ref.shape[1]
    zh, core, y = flag_ref[0], flag_ref[1], flag_ref[2]
    for ref, a, b in (
        (near_ref, 0, 0),
        (far_ref, 1, 0),
        (near_other_ref, 0, 1),
        (far_other_ref, 1, 1),
    ):
        slot = lax.bitwise_xor(zh, a) * 2 + lax.bitwise_xor(core, b)
        rows = pl.ds(pl.multiple_of(slot * cols, 16), cols)
        for k in range(groups):
            out_ref[lax.rem(y + groups - k, groups), rows, :] = ref[k]


def join(flags, pieces):
    groups, cols, depth = pieces[0].shape
    return pl.pallas_call(
        join_body,
        out_shape=jax.ShapeDtypeStruct((groups, 4 * cols, depth), bf16),
        in_specs=[SMEM] + [VMEM] * 4,
        out_specs=VMEM,
        cost_estimate=cost(0, 16 * groups * cols * depth),
        compiler_params=grant(10),
        name="join",
    )(flags, *pieces)


def project_body(sizes, ho_ref, w_ref, out_ref, lhs_ref):
    x_size, za_size, zb_size = sizes
    y_size, toks = w_ref.shape[0], ho_ref.shape[1]
    rows = toks // (za_size * zb_size)
    acc = None
    for y in range(y_size):
        for zb in range(zb_size):
            for za in range(za_size):
                for x in range(x_size):
                    at = ((zb * za_size + za) * x_size + x) * rows
                    src = (za * zb_size + zb) * rows
                    lhs_ref[at : at + rows] = ho_ref[x * y_size + y, src : src + rows]
        d = lax.dot_general(
            w_ref[y], lhs_ref[...], (((1,), (1,)), ((), ())), preferred_element_type=f32
        )
        acc = d if acc is None else acc + d
    acc = acc.astype(bf16)
    width = out_ref.shape[2]
    for zb in range(zb_size):
        out_ref[zb] = acc[:, zb * width : (zb + 1) * width]


def project(ho, w, x_size, za_size, zb_size):
    members, toks, depth = ho.shape
    cols = w.shape[1]
    lhs_rows = x_size * toks
    return pl.pallas_call(
        functools.partial(project_body, (x_size, za_size, zb_size)),
        out_shape=jax.ShapeDtypeStruct((zb_size, cols, lhs_rows // zb_size), bf16),
        in_specs=[VMEM, VMEM],
        out_specs=VMEM,
        scratch_shapes=[pltpu.VMEM((lhs_rows, depth), bf16)],
        cost_estimate=cost(2 * members * toks * depth * cols, 2 * members * toks * depth),
        compiler_params=grant(12),
        name="project",
    )(ho, w)


def layer(q_nope, q_rope, w_uk, w_uv, w_o, cache_kv, new_kv, block_order, cache_lengths):
    tok_rows, heads_here, nope_width = q_nope.shape
    latent_width = w_uk.shape[2]
    x_size, zh_size, core_size, za_size, zb_size, y_size = (
        lax.axis_size(a) for a in ("x", "zh", "core", "za", "zb", "y")
    )
    x_at, zh_at, core_at, y_at = (lax.axis_index(a) for a in ("x", "zh", "core", "y"))
    scale = float(nope_width + q_rope.shape[2]) ** (-0.5) * 1.4426950408889634

    copies, quarter = pack(cache_kv.T, new_kv.T, latent_width, x_size, y_at, y_size)
    line = zh_size * za_size * zb_size
    mirror = [(i, line - 1 - i) for i in range(line)]
    far_quarter = lax.ppermute(quarter, ("zh", "za", "zb"), mirror)

    value_rows, col_count = w_o.shape
    cols = col_count // y_size
    w_t = w_o.T.reshape(y_size, cols, value_rows)
    parts = [lax.dynamic_index_in_dim(w_t, y_at, 0)]
    for k in range(1, y_size):
        part = lax.dynamic_index_in_dim(w_t, (y_at + k) % y_size, 0)
        parts.append(lax.ppermute(part, "y", [(i, (i + k) % y_size) for i in range(y_size)]))
    w_t = jnp.concatenate(parts, axis=0)
    near = lax.all_to_all(copies, "x", 0, 0, tiled=False)
    far = spread(far_quarter, ("x", "y"))
    far = far.reshape(x_size, -1, tok_rows)
    w_far = lax.ppermute(w_t, "zh", swap)
    near_other = lax.ppermute(near, "core", swap)
    far_other = lax.ppermute(far, "core", swap)
    w_other = lax.ppermute(w_t, "core", swap)
    w_far_other = lax.ppermute(w_far, "core", swap)

    ql = jnp.einsum("thn,hnc->htc", q_nope, w_uk, preferred_element_type=f32).astype(bf16)
    ql = ql.reshape(heads_here * tok_rows, latent_width)
    rope = jnp.transpose(q_rope, (1, 0, 2))
    blank = jnp.zeros_like(rope)
    qr = jnp.stack([jnp.concatenate([rope, blank], axis=2), jnp.concatenate([blank, rope], axis=2)])
    qr = qr.reshape(2, heads_here * tok_rows, -1)
    ctx_count = x_size * zh_size * core_size
    shard_ids = jnp.arange(ctx_count, dtype=jnp.int32)
    own_ctx = (x_at * zh_size + zh_at) * core_size + core_at
    own_block = jnp.sum(jnp.where(shard_ids == own_ctx, block_order, 0))

    def of_piece(zh_flip, core_flip):
        column = jnp.arange(x_size * tok_rows, dtype=jnp.int32) // tok_rows
        owner = (column * zh_size + (zh_at ^ zh_flip)) * core_size + (core_at ^ core_flip)
        hit = owner[:, None] == shard_ids[None, :]
        limit = jnp.sum(jnp.where(hit, cache_lengths[None, :], 0), axis=1)
        block = jnp.sum(jnp.where(hit, block_order[None, :], 0), axis=1)
        return limit, (block - own_block) * tok_rows

    tables = [of_piece(a, b) for a in range(2) for b in range(2)]
    limits = jnp.stack([t[0] for t in tables])
    where = jnp.stack([t[1] for t in tables])

    pair = (near, near_other)
    state = attend(ql, qr, limits[:2], where[:2], pair, scale, heads_here)
    state = attend(ql, qr, limits[2:3], where[2:3], (far,), scale, heads_here, state)
    head_out = attend(
        ql, qr, limits[3:], where[3:], (far_other,), scale, heads_here, state, w_uv, x_size * y_size
    )

    gathered = lax.all_to_all(head_out, ("x", "y"), 0, 0, tiled=False)
    flags = jnp.stack([zh_at, core_at, y_at]).astype(jnp.int32)
    w_all = join(flags, (w_t, w_far, w_other, w_far_other))
    partial = project(gathered, w_all, x_size, za_size, zb_size)

    rows_out = tok_rows // (za_size * zb_size * y_size)
    width = partial.shape[1]
    got = lax.all_to_all(partial, "zb", 0, 0, tiled=False)
    partial = jnp.sum(got.astype(f32), axis=0).astype(bf16).T
    partial = partial.reshape(za_size * x_size * y_size, rows_out, width)
    got = lax.all_to_all(partial, ("za", "x", "y"), 0, 0, tiled=False)
    got = got.reshape(za_size, x_size, y_size, rows_out, zh_size * core_size, cols)
    mixed = jnp.sum(got.astype(f32), axis=0).astype(bf16)
    mixed = jnp.transpose(mixed, (2, 0, 3, 1, 4))
    return mixed.reshape(rows_out, -1)


def solution(mesh):
    axes = ("x", "zh", "core", "za", "zb", "y")
    fine = Mesh(mesh.devices.reshape(4, 2, 2, 2, 4, 4), axes)
    ctx, head = axes[:3], axes[3:]
    in_specs = (
        P(ctx, head, None),
        P(ctx, head, None),
        P(head, None, None),
        P(head, None, None),
        P(head, ctx),
        P(ctx, None),
        P(ctx, None),
        P(),
        P(),
    )
    out_specs = P(axes, None)
    return jax.shard_map(layer, mesh=fine, in_specs=in_specs, out_specs=out_specs, check_vma=False)
```

time: 238 us -> 209 us (0.88)
  Pallas kernels: 33.8 us -> 15.7 us
  waiting for transfers between devices: 82.5 us -> 64.4 us
  blocking collectives: 38.5 us -> 56 us
  local copies, waits for them, and re-layouts: 15.4 us -> 8.52 us
  other arithmetic: 7.87 us -> 3.39 us
    ppermute x1, waiting for transfers between devices: 43 us -> 22.3 us  [layer(): w_far = lax.ppermute(w_t, 'zh', swap)]
    all_to_all x1, blocking collectives: 16 us -> 32.3 us  [layer(): got = lax.all_to_all(partial, 'zb', 0, 0, tiled=False)]
    pallas_call x6 -> x5, Pallas kernels: 31 us -> 15.1 us  [the longest x3 12.7 us: attend(): pl.pallas_call(functools.partial(attend_body, first, last, len(keys), hea...]
    all_to_all x0 -> x1, starting transfers between devices: none -> 6.35 us  [layer(): gathered = lax.all_to_all(head_out, ('x', 'y'), 0, 0, tiled=False)]
    all_to_all x2 -> x1, starting transfers between devices: 13.9 us -> 7.59 us  [spread(): return lax.all_to_all(copies, axes, 0, 0, tiled=False)]
    ppermute x1, starting transfers between devices: 7.31 us -> 10.7 us  [layer(): w_far = lax.ppermute(w_t, 'zh', swap)]
    broadcast_in_dim x2 -> x1, local copies, waits for them, and re-layouts: 3.63 us -> 1.17 us  [spread(): copies = jnp.broadcast_to(value[None], (count,) + value.shape)]
    unnamed x29 -> x25, local copies, waits for them, and re-layouts: 7.79 us -> 6.08 us
  transfers between devices with their start and end apart: 12 -> 12, of which waited for: 7 -> 6; matrix products, arithmetic and copies ran while one was open for 4% -> 2% of each run, Pallas kernels for 8% -> 4%
where the time goes in v3:
time: 209 us; the launch traced here: 207 us
  waiting for transfers between devices  64.4 us (31%)
  starting transfers between devices  58.7 us (28%)
  blocking collectives  56 us (27%)
  Pallas kernels  15.7 us (8%)
  local copies, waits for them, and re-layouts  8.52 us (4%)
  other arithmetic  3.39 us (2%)
    all_to_all x1, blocking collectives, layer(): got = lax.all_to_all(partial, 'zb', 0, 0, tiled=False)  32.3 us
    all_to_all x1, blocking collectives, layer(): got = lax.all_to_all(partial, ('za', 'x', 'y'), 0, 0, tiled=False)  23.8 us
    ppermute x1, waiting for transfers between devices, layer(): w_far = lax.ppermute(w_t, 'zh', swap)  22.3 us
    ppermute x3, waiting for transfers between devices, layer(): lax.ppermute(part, 'y', [(i, (i + k) % y_size) for i in range(y_size)])  21.6 us
    pallas_call x3, Pallas kernels, attend(): pl.pallas_call(functools.partial(attend_body, first, last, len(keys), hea...  12.7 us
    all_to_all x1, waiting for transfers between devices, spread(): return lax.all_to_all(copies, axes, 0, 0, tiled=False)  12.5 us
    ppermute x1, starting transfers between devices, layer(): w_far = lax.ppermute(w_t, 'zh', swap)  10.7 us
    ppermute x3, starting transfers between devices, layer(): lax.ppermute(part, 'y', [(i, (i + k) % y_size) for i in range(y_size)])  10.1 us
  transfers between devices with their start and end apart: 12, of which 6 were waited for; matrix products, arithmetic and copies ran while one was open for 2% of the time, Pallas kernels for 4%

profile of v3, /device:TPU:6, one launch (start us, length us, event | category | flops | bytes accessed | tf_op | source)
XLA Modules:
  0.0 207.4 jit_solution(2038782369350245653)
XLA Ops:
  0.0 1.0 copy-done.5
  1.0 0.9 copy-done.6
  1.9 1.2 pack.1
  3.1 9.5 %all-to-all-start.1 = ((bf16[4,1152,128]{2,1,0:T(8,128)(2,1)}), bf16[4,1152,128]{2,1,0:T(8,128)(2,1)S(1)}, u32[]{:S(2)}, u32[]{:S(2)}) async-start(bf16[4,1152,128]{2,1,0:T(8,128)(2,1)} %get-tuple-element.14), calls=%async_computation.1 | async-start | bytes 2359296 | tf_op jit(solution)/shard_map/all_to_all | solution.py:259
  12.5 6.8 %collective-permute-start = (bf16[288,128]{1,0:T(8,128)(2,1)S(1)}, bf16[288,128]{1,0:T(8,128)(2,1)S(1)}, u32[]{:S(2)}, u32[]{:S(2)}) collective-permute-start(bf16[288,128]{1,0:T(8,128)(2,1)S(1)} %get-tuple-element.13), channel_id=1, source_target_pairs={{0,92},{4,88},{8,84},{12,80},{16,76},{20,72},{24,68},{28,64},{64,2... | collective-permute-start | bytes 221192 | tf_op jit(solution)/shard_map/ppermute | solution.py:249
  19.5 6.3 %collective-permute-done = bf16[288,128]{1,0:T(8,128)(2,1)S(1)} collective-permute-done((bf16[288,128]{1,0:T(8,128)(2,1)S(1)}, bf16[288,128]{1,0:T(8,128)(2,1)S(1)}, u32[]{:S(2)}, u32[]{:S(2)}) %collective-permute-start) | collective-permute-done | bytes 73760 | tf_op jit(solution)/shard_map/ppermute | solution.py:249
  25.8 1.2 broadcast_in_dim.73
  27.0 7.6 %all-to-all-start = ((bf16[16,288,128]{2,1,0:T(8,128)(2,1)}), bf16[16,288,128]{2,1,0:T(8,128)(2,1)S(1)}, u32[]{:S(2)}, u32[]{:S(2)}) async-start(bf16[16,288,128]{2,1,0:T(8,128)(2,1)} %broadcast_in_dim.73), calls=%async_computation | async-start | bytes 2359296 | tf_op jit(solution)/shard_map/all_to_all | solution.py:23
  36.1 1.9 collective-permute-start.2
  38.6 12.5 %all-to-all-done = bf16[16,288,128]{2,1,0:T(8,128)(2,1)S(1)} async-done(((bf16[16,288,128]{2,1,0:T(8,128)(2,1)}), bf16[16,288,128]{2,1,0:T(8,128)(2,1)S(1)}, u32[]{:S(2)}, u32[]{:S(2)}) %all-to-all-start) | async-done | bytes 1179680 | tf_op jit(solution)/shard_map/all_to_all | solution.py:23
  51.0 1.9 collective-permute-start.1
  54.5 5.0 %attend.3 = (f32[512,128]{1,0:T(8,128)S(1)}, f32[512,128]{1,0:T(8,128)S(1)}, f32[512,512]{1,0:T(8,128)S(1)}) custom-call(bf16[512,512]{1,0:T(8,128)(2,1)S(1)} %bitcast.24, bf16[2,512,128]{2,1,0:T(8,128)(2,1)S(1)} %pad_maximum_fusion.1.refs_1_, s32[2,512]{1,0:T(2,128)S(1)} %pad_add_fusion.refs_2_, s32[2,512]{1,0:T(2,128)S(1)} %pad_add_fusion.1.refs_3_, ...), custom_call_target="tpu_custom_call" | custom-call | flops 2147483648 | bytes 4194304 | tf_op jit(solution)/shard_map/attend/pallas_call | solution.py:159
  59.5 2.5 %attend.4 = (f32[512,128]{1,0:T(8,128)S(1)}, f32[512,128]{1,0:T(8,128)S(1)}, f32[512,512]{1,0:T(8,128)S(1)}) custom-call(bf16[512,512]{1,0:T(8,128)(2,1)S(1)} %bitcast.25, bf16[2,512,128]{2,1,0:T(8,128)(2,1)S(1)} %pad_maximum_fusion.1.refs_1_, s32[1,512]{1,0:T(1,128)S(1)} %bitcast.33, s32[1,512]{1,0:T(1,128)S(1)} %bitcast.34, ...), custom_call_target="tpu_custom_call" | custom-call | flops 1073741824 | bytes 2097152 | tf_op jit(solution)/shard_map/attend/pallas_call | solution.py:159
  62.0 5.2 %attend.5 = bf16[16,128,512]{2,1,0:T(8,128)(2,1)S(1)} custom-call(bf16[512,512]{1,0:T(8,128)(2,1)S(1)} %bitcast.26, bf16[2,512,128]{2,1,0:T(8,128)(2,1)S(1)} %pad_maximum_fusion.1.refs_1_, s32[1,512]{1,0:T(1,128)S(1)} %bitcast.31, s32[1,512]{1,0:T(1,128)S(1)} %bitcast.32, bf16[4,1152,128]{2,1,0:T(8,128)(2,1)S(1)} %collective-permute-done.1.refs_4_, ...), custom_call_target="tpu_custom_call" | custom-call | flops 1073741824 | bytes 2097152 | tf_op jit(solution)/shard_map/attend/pallas_call | solution.py:159
  67.2 1.3 copy-done.1
  68.6 6.4 %all-to-all-start.2 = ((bf16[16,128,512]{2,1,0:T(8,128)(2,1)}), bf16[16,128,512]{2,1,0:T(8,128)(2,1)S(1)}, u32[]{:S(2)}, u32[]{:S(2)}) async-start(bf16[16,128,512]{2,1,0:T(8,128)(2,1)} %copy-done.1), calls=%async_computation.2 | async-start | bytes 4194304 | tf_op jit(solution)/shard_map/all_to_all | solution.py:298
  75.0 4.6 %collective-permute-start.5 = (bf16[1,112,512]{2,1,0:T(8,128)(2,1)S(1)}, bf16[1,112,512]{2,1,0:T(8,128)(2,1)S(1)}, u32[]{:S(2)}, u32[]{:S(2)}) collective-permute-start(bf16[1,112,512]{2,1,0:T(8,128)(2,1)S(1)} %get-tuple-element.36), channel_id=1, source_target_pairs={{0,3},{1,0},{2,1},{3,2},{4,7},{5,4},{6,5},{7,6},{8,11},{9,8},{10,9... | collective-permute-start | bytes 344072 | tf_op jit(solution)/shard_map/ppermute | solution.py:257
  79.6 2.8 %collective-permute-start.4 = (bf16[1,112,512]{2,1,0:T(8,128)(2,1)S(1)}, bf16[1,112,512]{2,1,0:T(8,128)(2,1)S(1)}, u32[]{:S(2)}, u32[]{:S(2)}) collective-permute-start(bf16[1,112,512]{2,1,0:T(8,128)(2,1)S(1)} %get-tuple-element.37), channel_id=1, source_target_pairs={{0,2},{1,3},{2,0},{3,1},{4,6},{5,7},{6,4},{7,5},{8,10},{9,11},{10,... | collective-permute-start | bytes 344072 | tf_op jit(solution)/shard_map/ppermute | solution.py:257
  82.3 2.8 %collective-permute-start.3 = (bf16[1,112,512]{2,1,0:T(8,128)(2,1)S(1)}, bf16[1,112,512]{2,1,0:T(8,128)(2,1)S(1)}, u32[]{:S(2)}, u32[]{:S(2)}) collective-permute-start(bf16[1,112,512]{2,1,0:T(8,128)(2,1)S(1)} %get-tuple-element.38), channel_id=1, source_target_pairs={{0,1},{1,2},{2,3},{3,0},{4,5},{5,6},{6,7},{7,4},{8,9},{9,10},{10,1... | collective-permute-start | bytes 344072 | tf_op jit(solution)/shard_map/ppermute | solution.py:257
  85.1 20.3 %collective-permute-done.5 = bf16[1,112,512]{2,1,0:T(8,128)(2,1)S(1)} collective-permute-done((bf16[1,112,512]{2,1,0:T(8,128)(2,1)S(1)}, bf16[1,112,512]{2,1,0:T(8,128)(2,1)S(1)}, u32[]{:S(2)}, u32[]{:S(2)}) %collective-permute-start.5) | collective-permute-done | bytes 114720 | tf_op jit(solution)/shard_map/ppermute | solution.py:257
  105.4 1.3 collective-permute-done.3
  106.8 10.7 %collective-permute-start.6 = (bf16[4,112,512]{2,1,0:T(8,128)(2,1)S(1)}, bf16[4,112,512]{2,1,0:T(8,128)(2,1)S(1)}, u32[]{:S(2)}, u32[]{:S(2)}) collective-permute-start(bf16[4,112,512]{2,1,0:T(8,128)(2,1)S(1)} %pad_maximum_fusion.near_ref), channel_id=1, source_target_pairs={{0,64},{64,0},{1,65},{65,1},{2,66},{66,2},{3,67},{67,3},{4,68},{68... | collective-permute-start | bytes 1376264 | tf_op jit(solution)/shard_map/ppermute | solution.py:262
  117.5 1.9 collective-permute-start.7
  119.4 22.3 %collective-permute-done.6.far_ref = bf16[4,112,512]{2,1,0:T(8,128)(2,1)S(1)} collective-permute-done((bf16[4,112,512]{2,1,0:T(8,128)(2,1)S(1)}, bf16[4,112,512]{2,1,0:T(8,128)(2,1)S(1)}, u32[]{:S(2)}, u32[]{:S(2)}) %collective-permute-start.6) | collective-permute-done | bytes 458784 | tf_op jit(solution)/shard_map/ppermute | solution.py:262
  141.7 1.9 collective-permute-start.8
  143.7 1.7 collective-permute-done.8.far_other_ref
  146.1 1.2 copy-done.2
  147.4 1.5 copy-done.3
  148.8 1.1 project.1
  150.0 32.3 %all_to_all.25 = bf16[4,448,128]{2,1,0:T(8,128)(2,1)S(1)} all-to-all(bf16[4,448,128]{2,1,0:T(8,128)(2,1)S(1)} %project.1), channel_id=1, replica_groups=mesh['x'=4,'zh'=2,'core'=2,'za'=2,'zb'=4,'y'=4] {'zb'}, dimensions={0} | all-to-all | bytes 917504 | tf_op jit(solution)/shard_map/all_to_all | solution.py:305
  182.5 23.8 %all_to_all.26 = bf16[32,4,448]{2,1,0:T(4,128)(2,1)S(1)} all-to-all(bf16[32,4,448]{2,1,0:T(4,128)(2,1)S(1)} %reshape.117), channel_id=1, replica_groups=mesh['x'=4,'zh'=2,'core'=2,'za'=2,'zb'=4,'y'=4] {'za','x','y'}, dimensions={0} | all-to-all | bytes 229376 | tf_op jit(solution)/shard_map/all_to_all | solution.py:308
  206.6 0.8 reshape.119
  (49 shorter events, 5.0 us)
Async XLA Ops:
  0.0 54.2 %copy-start = (bf16[4,128,512]{2,1,0:T(8,128)(2,1)S(1)}, bf16[4,128,512]{2,1,0:T(8,128)(2,1)}, u32[]{:S(2)}) copy-start(bf16[4,128,512]{2,1,0:T(8,128)(2,1)} %param.11) | copy-start | bytes 1572868
  0.0 1.0 copy-start.5
  1.0 0.9 copy-start.6
  3.1 16.3 %copy-start.9 = (bf16[128,4,64]{0,2,1:T(8,128)(2,1)S(1)}, bf16[128,4,64]{0,2,1:T(8,128)(2,1)}, u32[]{:S(2)}) copy-start(bf16[128,4,64]{0,2,1:T(8,128)(2,1)} %param.10) | copy-start | bytes 196612
  3.1 22.7 %all-to-all-start.1 = ((bf16[4,1152,128]{2,1,0:T(8,128)(2,1)}), bf16[4,1152,128]{2,1,0:T(8,128)(2,1)S(1)}, u32[]{:S(2)}, u32[]{:S(2)}) async-start(bf16[4,1152,128]{2,1,0:T(8,128)(2,1)} %get-tuple-element.14), calls=%async_computation.1 | async-start | bytes 2359296 | tf_op jit(solution)/shard_map/all_to_all | solution.py:259
  12.5 13.3 %collective-permute-start = (bf16[288,128]{1,0:T(8,128)(2,1)S(1)}, bf16[288,128]{1,0:T(8,128)(2,1)S(1)}, u32[]{:S(2)}, u32[]{:S(2)}) collective-permute-start(bf16[288,128]{1,0:T(8,128)(2,1)S(1)} %get-tuple-element.13), channel_id=1, source_target_pairs={{0,92},{4,88},{8,84},{12,80},{16,76},{20,72},{24,68},{28,64},{64,2... | collective-permute-start | bytes 221192 | tf_op jit(solution)/shard_map/ppermute | solution.py:249
  27.0 7.6 %copy-start.10 = (s32[16]{0:T(128)S(1)}, s32[16]{0:T(128)}, u32[]{:S(2)}) copy-start(s32[16]{0:T(128)} %param.16) | copy-start | bytes 196
  27.0 8.2 %copy-start.11 = (s32[16]{0:T(128)S(1)}, s32[16]{0:T(128)}, u32[]{:S(2)}) copy-start(s32[16]{0:T(128)} %param.17) | copy-start | bytes 196
  27.0 27.2 %copy-start.8 = (bf16[128,4,128]{2,1,0:T(4,128)(2,1)S(1)}, bf16[128,4,128]{2,1,0:T(4,128)(2,1)}, u32[]{:S(2)}) copy-start(bf16[128,4,128]{2,1,0:T(4,128)(2,1)} %param.9) | copy-start | bytes 393220
  27.0 24.0 %all-to-all-start = ((bf16[16,288,128]{2,1,0:T(8,128)(2,1)}), bf16[16,288,128]{2,1,0:T(8,128)(2,1)S(1)}, u32[]{:S(2)}, u32[]{:S(2)}) async-start(bf16[16,288,128]{2,1,0:T(8,128)(2,1)} %broadcast_in_dim.73), calls=%async_computation | async-start | bytes 2359296 | tf_op jit(solution)/shard_map/all_to_all | solution.py:23
  36.1 18.4 %collective-permute-start.2 = (bf16[4,1152,128]{2,1,0:T(8,128)(2,1)S(1)}, bf16[4,1152,128]{2,1,0:T(8,128)(2,1)}, u32[]{:S(2)}, u32[]{:S(2)}) collective-permute-start(bf16[4,1152,128]{2,1,0:T(8,128)(2,1)S(1)} %all-to-all-done.1.refs_4_), channel_id=1, source_target_pairs={{0,32},{32,0},{1,33},{33,1},{2,34},{34,2},{3,35},{35,3},{4,36},{36... | collective-permute-start | bytes 3538952 | tf_op jit(solution)/shard_map/ppermute | solution.py:263
  51.0 10.9 %collective-permute-start.1 = (bf16[4,1152,128]{2,1,0:T(8,128)(2,1)S(1)}, bf16[4,1152,128]{2,1,0:T(8,128)(2,1)S(1)}, u32[]{:S(2)}, u32[]{:S(2)}) collective-permute-start(bf16[4,1152,128]{2,1,0:T(8,128)(2,1)S(1)} %bitcast.27), channel_id=1, source_target_pairs={{0,32},{32,0},{1,33},{33,1},{2,34},{34,2},{3,35},{35,3},{4,36},{36... | collective-permute-start | bytes 3538952 | tf_op jit(solution)/shard_map/ppermute | solution.py:264
  59.5 2.5 %copy-start.4 = (bf16[4,512,128]{2,1,0:T(8,128)(2,1)S(1)}, bf16[4,512,128]{2,1,0:T(8,128)(2,1)}, u32[]{:S(2)}) copy-start(bf16[4,512,128]{2,1,0:T(8,128)(2,1)} %refs_8_.1) | copy-start | bytes 1572868
  67.2 1.3 copy-start.1
  68.6 6.4 %copy-start.7 = (bf16[512,448]{0,1:T(8,128)(2,1)S(1)}, bf16[512,448]{0,1:T(8,128)(2,1)}, u32[]{:S(2)}) copy-start(bf16[512,448]{0,1:T(8,128)(2,1)} %param.13) | copy-start | bytes 1376260
  68.6 78.8 %all-to-all-start.2 = ((bf16[16,128,512]{2,1,0:T(8,128)(2,1)}), bf16[16,128,512]{2,1,0:T(8,128)(2,1)S(1)}, u32[]{:S(2)}, u32[]{:S(2)}) async-start(bf16[16,128,512]{2,1,0:T(8,128)(2,1)} %copy-done.1), calls=%async_computation.2 | async-start | bytes 4194304 | tf_op jit(solution)/shard_map/all_to_all | solution.py:298
  75.0 30.4 %collective-permute-start.5 = (bf16[1,112,512]{2,1,0:T(8,128)(2,1)S(1)}, bf16[1,112,512]{2,1,0:T(8,128)(2,1)S(1)}, u32[]{:S(2)}, u32[]{:S(2)}) collective-permute-start(bf16[1,112,512]{2,1,0:T(8,128)(2,1)S(1)} %get-tuple-element.36), channel_id=1, source_target_pairs={{0,3},{1,0},{2,1},{3,2},{4,7},{5,4},{6,5},{7,6},{8,11},{9,8},{10,9... | collective-permute-start | bytes 344072 | tf_op jit(solution)/shard_map/ppermute | solution.py:257
  79.6 25.8 %collective-permute-start.4 = (bf16[1,112,512]{2,1,0:T(8,128)(2,1)S(1)}, bf16[1,112,512]{2,1,0:T(8,128)(2,1)S(1)}, u32[]{:S(2)}, u32[]{:S(2)}) collective-permute-start(bf16[1,112,512]{2,1,0:T(8,128)(2,1)S(1)} %get-tuple-element.37), channel_id=1, source_target_pairs={{0,2},{1,3},{2,0},{3,1},{4,6},{5,7},{6,4},{7,5},{8,10},{9,11},{10,... | collective-permute-start | bytes 344072 | tf_op jit(solution)/shard_map/ppermute | solution.py:257
  82.3 24.4 %collective-permute-start.3 = (bf16[1,112,512]{2,1,0:T(8,128)(2,1)S(1)}, bf16[1,112,512]{2,1,0:T(8,128)(2,1)S(1)}, u32[]{:S(2)}, u32[]{:S(2)}) collective-permute-start(bf16[1,112,512]{2,1,0:T(8,128)(2,1)S(1)} %get-tuple-element.38), channel_id=1, source_target_pairs={{0,1},{1,2},{2,3},{3,0},{4,5},{5,6},{6,7},{7,4},{8,9},{9,10},{10,1... | collective-permute-start | bytes 344072 | tf_op jit(solution)/shard_map/ppermute | solution.py:257
  106.8 34.9 %collective-permute-start.6 = (bf16[4,112,512]{2,1,0:T(8,128)(2,1)S(1)}, bf16[4,112,512]{2,1,0:T(8,128)(2,1)S(1)}, u32[]{:S(2)}, u32[]{:S(2)}) collective-permute-start(bf16[4,112,512]{2,1,0:T(8,128)(2,1)S(1)} %pad_maximum_fusion.near_ref), channel_id=1, source_target_pairs={{0,64},{64,0},{1,65},{65,1},{2,66},{66,2},{3,67},{67,3},{4,68},{68... | collective-permute-start | bytes 1376264 | tf_op jit(solution)/shard_map/ppermute | solution.py:262
  117.5 26.3 %collective-permute-start.7 = (bf16[4,112,512]{2,1,0:T(8,128)(2,1)S(1)}, bf16[4,112,512]{2,1,0:T(8,128)(2,1)S(1)}, u32[]{:S(2)}, u32[]{:S(2)}) collective-permute-start(bf16[4,112,512]{2,1,0:T(8,128)(2,1)S(1)} %pad_maximum_fusion.near_ref), channel_id=1, source_target_pairs={{0,32},{32,0},{1,33},{33,1},{2,34},{34,2},{3,35},{35,3},{4,36},{36... | collective-permute-start | bytes 1376264 | tf_op jit(solution)/shard_map/ppermute | solution.py:265
  141.7 3.7 %collective-permute-start.8 = (bf16[4,112,512]{2,1,0:T(8,128)(2,1)S(1)}, bf16[4,112,512]{2,1,0:T(8,128)(2,1)S(1)}, u32[]{:S(2)}, u32[]{:S(2)}) collective-permute-start(bf16[4,112,512]{2,1,0:T(8,128)(2,1)S(1)} %collective-permute-done.6.far_ref), channel_id=1, source_target_pairs={{0,32},{32,0},{1,33},{33,1},{2,34},{34,2},{3,35},{35,3},{4,36},{36... | collective-permute-start | bytes 1376264 | tf_op jit(solution)/shard_map/ppermute | solution.py:266
  146.1 1.2 copy-start.2
  147.3 1.5 copy-start.3

commit v4 on v3

--- a/solution.py
+++ b/solution.py
@@ -31,7 +31,7 @@
     return pl.CostEstimate(flops=flops, bytes_accessed=nbytes, transcendentals=trans)
 
 
-def pack_body(latent_width, at_ref, cache_ref, new_ref, copies_ref, part_ref, row_ref):
+def pack_body(latent_width, at_ref, cache_ref, new_ref, row_ref, part_ref):
     rope = cache_ref.shape[0] - latent_width
     row_ref[:latent_width] = cache_ref[:latent_width]
     row_ref[latent_width : 2 * latent_width] = new_ref[:latent_width]
@@ -39,23 +39,20 @@
     row_ref[2 * latent_width + rope :] = new_ref[latent_width:]
     rows = part_ref.shape[0]
     part_ref[...] = row_ref[pl.ds(pl.multiple_of(at_ref[0] * rows, 16), rows), :]
-    for copy in range(copies_ref.shape[0]):
-        copies_ref[copy] = row_ref[...]
-
-
-def pack(cache, new, latent_width, copies, part, parts):
+
+
+def pack(cache, new, latent_width, part, parts):
     width, slots = cache.shape
     depth = 2 * width
     return pl.pallas_call(
         functools.partial(pack_body, latent_width),
         out_shape=(
-            jax.ShapeDtypeStruct((copies, depth, slots), bf16),
+            jax.ShapeDtypeStruct((depth, slots), bf16),
             jax.ShapeDtypeStruct((depth // parts, slots), bf16),
         ),
         in_specs=[SMEM, VMEM, VMEM],
         out_specs=(VMEM, VMEM),
-        scratch_shapes=[pltpu.VMEM((depth, slots), bf16)],
-        cost_estimate=cost(0, 2 * (copies + 2) * depth * slots),
+        cost_estimate=cost(0, 6 * depth * slots),
         compiler_params=grant(6),
         name="pack",
     )(part.astype(jnp.int32).reshape(1), cache, new)
@@ -82,37 +79,44 @@
     def features(p, start, stop):
         return jnp.concatenate([keys[p][s, start:stop, :] for s in range(shards)], axis=1)
 
-    scores = []
-    for p in range(pieces):
-        rope = features(p, 2 * width, depth)
-        for kind in range(2):
+    ms, totals, accs = [], [], []
+    for r in range(0, rows, 256):
+        rs = slice(r, r + 256)
+        scores = []
+        for p in range(pieces):
+            rope = features(p, 2 * width, depth)
+            for kind in range(2):
+                lat = features(p, kind * width, (kind + 1) * width)
+                s = jnp.dot(ql_ref[rs], lat, preferred_element_type=f32)
+                s = s + jnp.dot(qr_ref[kind, rs], rope, preferred_element_type=f32)
+                if kind:
+                    seen = where_ref[p : p + 1, :] + slot <= tok[rs]
+                else:
+                    seen = jnp.broadcast_to(slot < limit_ref[p : p + 1, :], s.shape)
+                scores.append(jnp.where(seen, s, neg_large))
+        top = jnp.max(functools.reduce(jnp.maximum, scores), axis=1, keepdims=True)
+        if first:
+            m, total, acc = top, None, None
+        else:
+            m_old = m_in[rs, :1]
+            m = jnp.maximum(top, m_old)
+            keep = jnp.exp2((m_old - m) * scale)
+            total = l_in[rs, :1] * keep
+            acc = acc_in[rs] * keep
+        sums = None
+        for at, s in enumerate(scores):
+            p, kind = at // 2, at % 2
             lat = features(p, kind * width, (kind + 1) * width)
-            s = jnp.dot(ql_ref[...], lat, preferred_element_type=f32)
-            s = s + jnp.dot(qr_ref[kind], rope, preferred_element_type=f32)
-            if kind:
-                seen = where_ref[p : p + 1, :] + slot <= tok
-            else:
-                seen = jnp.broadcast_to(slot < limit_ref[p : p + 1, :], s.shape)
-            scores.append(jnp.where(seen, s, neg_large))
-    top = jnp.max(functools.reduce(jnp.maximum, scores), axis=1, keepdims=True)
-    if first:
-        m, total, acc = top, None, None
-    else:
-        m_old = m_in[:, :1]
-        m = jnp.maximum(top, m_old)
-        keep = jnp.exp2((m_old - m) * scale)
-        total = l_in[:, :1] * keep
-        acc = acc_in[...] * keep
-    sums = None
-    for at, s in enumerate(scores):
-        p, kind = at // 2, at % 2
-        lat = features(p, kind * width, (kind + 1) * width)
-        e = jnp.exp2((s - m) * scale)
-        sums = e if sums is None else sums + e
-        d = lax.dot_general(e.astype(bf16), lat, (((1,), (1,)), ((), ())), preferred_element_type=f32)
-        acc = d if acc is None else acc + d
-    sums = jnp.sum(sums, axis=1, keepdims=True)
-    total = sums if total is None else total + sums
+            e = jnp.exp2((s - m) * scale)
+            sums = e if sums is None else sums + e
+            d = lax.dot_general(e.astype(bf16), lat, (((1,), (1,)), ((), ())), preferred_element_type=f32)
+            acc = d if acc is None else acc + d
+        sums = jnp.sum(sums, axis=1, keepdims=True)
+        total = sums if total is None else total + sums
+        ms.append(m)
+        totals.append(total)
+        accs.append(acc)
+    m, total, acc = (jnp.concatenate(v, axis=0) for v in (ms, totals, accs))
     if last:
         out_ref, hold_ref, sem = refs
         out = (acc / total).astype(bf16)
@@ -147,13 +151,13 @@
     if last:
         args.append(w_uv)
         wide = heads * w_uv.shape[2]
-        out_shape = jax.ShapeDtypeStruct((copies, toks, wide), bf16)
+        out_shape = pltpu.HBM((copies, toks, wide), bf16)
         scratch = [pltpu.VMEM((toks, wide), bf16), pltpu.SemaphoreType.DMA((copies,))]
     else:
         out_shape = (
-            jax.ShapeDtypeStruct((rows, 128), f32),
-            jax.ShapeDtypeStruct((rows, 128), f32),
-            jax.ShapeDtypeStruct((rows, width), f32),
+            pltpu.VMEM((rows, 128), f32),
+            pltpu.VMEM((rows, 128), f32),
+            pltpu.VMEM((rows, width), f32),
         )
     count = 2 * len(keys) * keys[0].shape[0] * keys[0].shape[2]
     return pl.pallas_call(
@@ -169,8 +173,8 @@
 
 
 def join_body(flag_ref, near_ref, far_ref, near_other_ref, far_other_ref, out_ref):
-    groups, cols = near_ref.shape[0], near_ref.shape[1]
-    zh, core, y = flag_ref[0], flag_ref[1], flag_ref[2]
+    cols = near_ref.shape[1]
+    zh, core = flag_ref[0], flag_ref[1]
     for ref, a, b in (
         (near_ref, 0, 0),
         (far_ref, 1, 0),
@@ -179,15 +183,14 @@
     ):
         slot = lax.bitwise_xor(zh, a) * 2 + lax.bitwise_xor(core, b)
         rows = pl.ds(pl.multiple_of(slot * cols, 16), cols)
-        for k in range(groups):
-            out_ref[lax.rem(y + groups - k, groups), rows, :] = ref[k]
+        out_ref[:, rows, :] = ref[...]
 
 
 def join(flags, pieces):
     groups, cols, depth = pieces[0].shape
     return pl.pallas_call(
         join_body,
-        out_shape=jax.ShapeDtypeStruct((groups, 4 * cols, depth), bf16),
+        out_shape=pltpu.VMEM((groups, 4 * cols, depth), bf16),
         in_specs=[SMEM] + [VMEM] * 4,
         out_specs=VMEM,
         cost_estimate=cost(0, 16 * groups * cols * depth),
@@ -243,7 +246,7 @@
     x_at, zh_at, core_at, y_at = (lax.axis_index(a) for a in ("x", "zh", "core", "y"))
     scale = float(nope_width + q_rope.shape[2]) ** (-0.5) * 1.4426950408889634
 
-    copies, quarter = pack(cache_kv.T, new_kv.T, latent_width, x_size, y_at, y_size)
+    own, quarter = pack(cache_kv.T, new_kv.T, latent_width, y_at, y_size)
     line = zh_size * za_size * zb_size
     mirror = [(i, line - 1 - i) for i in range(line)]
     far_quarter = lax.ppermute(quarter, ("zh", "za", "zb"), mirror)
@@ -251,12 +254,13 @@
     value_rows, col_count = w_o.shape
     cols = col_count // y_size
     w_t = w_o.T.reshape(y_size, cols, value_rows)
-    parts = [lax.dynamic_index_in_dim(w_t, y_at, 0)]
-    for k in range(1, y_size):
-        part = lax.dynamic_index_in_dim(w_t, (y_at + k) % y_size, 0)
-        parts.append(lax.ppermute(part, "y", [(i, (i + k) % y_size) for i in range(y_size)]))
-    w_t = jnp.concatenate(parts, axis=0)
-    near = lax.all_to_all(copies, "x", 0, 0, tiled=False)
+    w_t = lax.all_to_all(w_t, "y", 0, 0, tiled=False)
+    near_from = [x_at]
+    near = [own]
+    for k in (1, x_size - 1, *range(2, x_size - 1)):
+        near.append(lax.ppermute(own, "x", [(i, (i + k) % x_size) for i in range(x_size)]))
+        near_from.append((x_at - k) % x_size)
+    near = jnp.stack(near)
     far = spread(far_quarter, ("x", "y"))
     far = far.reshape(x_size, -1, tok_rows)
     w_far = lax.ppermute(w_t, "zh", swap)
@@ -276,8 +280,11 @@
     own_ctx = (x_at * zh_size + zh_at) * core_size + core_at
     own_block = jnp.sum(jnp.where(shard_ids == own_ctx, block_order, 0))
 
+    near_x = jnp.repeat(jnp.stack(near_from), tok_rows, total_repeat_length=x_size * tok_rows)
+    far_x = jnp.arange(x_size * tok_rows, dtype=jnp.int32) // tok_rows
+
     def of_piece(zh_flip, core_flip):
-        column = jnp.arange(x_size * tok_rows, dtype=jnp.int32) // tok_rows
+        column = far_x if zh_flip else near_x
         owner = (column * zh_size + (zh_at ^ zh_flip)) * core_size + (core_at ^ core_flip)
         hit = owner[:, None] == shard_ids[None, :]
         limit = jnp.sum(jnp.where(hit, cache_lengths[None, :], 0), axis=1)
@@ -296,7 +303,7 @@
     )
 
     gathered = lax.all_to_all(head_out, ("x", "y"), 0, 0, tiled=False)
-    flags = jnp.stack([zh_at, core_at, y_at]).astype(jnp.int32)
+    flags = jnp.stack([zh_at, core_at]).astype(jnp.int32)
     w_all = join(flags, (w_t, w_far, w_other, w_far_other))
     partial = project(gathered, w_all, x_size, za_size, zb_size)
 

time: 209 us -> 182 us (0.87)
  blocking collectives: 56 us -> 46 us
  waiting for transfers between devices: 64.4 us -> 55 us
  starting transfers between devices: 58.7 us -> 52.7 us
  Pallas kernels: 15.7 us -> 13 us
    ppermute x3, waiting for transfers between devices: 21.6 us -> 0.01 us  [layer(): lax.ppermute(own, 'x', [(i, (i + k) % x_size) for i in range(x_size)])]
    ppermute x1, waiting for transfers between devices: 22.3 us -> 36.3 us  [layer(): w_far = lax.ppermute(w_t, 'zh', swap)]
    all_to_all x1, blocking collectives: 32.3 us -> 20.5 us  [layer(): got = lax.all_to_all(partial, 'zb', 0, 0, tiled=False)]
    all_to_all x1, starting transfers between devices: 9.45 us -> 3.47 us  [layer(): w_t = lax.all_to_all(w_t, 'y', 0, 0, tiled=False)]
    ppermute x1, starting transfers between devices: 10.7 us -> 5.61 us  [layer(): w_far = lax.ppermute(w_t, 'zh', swap)]
    ppermute x3, starting transfers between devices: 10.1 us -> 13 us  [layer(): lax.ppermute(own, 'x', [(i, (i + k) % x_size) for i in range(x_size)])]
    unnamed x25 -> x21, local copies, waits for them, and re-layouts: 6.08 us -> 4.77 us
  transfers between devices with their start and end apart: 12 -> 12, of which waited for: 6 -> 4; matrix products, arithmetic and copies ran while one was open for 2% -> 3% of each run, Pallas kernels for 4% -> 7%
where the time goes in v4:
time: 182 us; the launch traced here: 179 us
  waiting for transfers between devices  55 us (30%)
  starting transfers between devices  52.7 us (29%)
  blocking collectives  46 us (25%)
  Pallas kernels  13 us (7%)
  local copies, waits for them, and re-layouts  7.15 us (4%)
  other arithmetic  4.57 us (3%)
    ppermute x1, waiting for transfers between devices, layer(): w_far = lax.ppermute(w_t, 'zh', swap)  36.3 us
    all_to_all x1, blocking collectives, layer(): got = lax.all_to_all(partial, ('za', 'x', 'y'), 0, 0, tiled=False)  25.5 us
    all_to_all x1, blocking collectives, layer(): got = lax.all_to_all(partial, 'zb', 0, 0, tiled=False)  20.5 us
    ppermute x3, starting transfers between devices, layer(): lax.ppermute(own, 'x', [(i, (i + k) % x_size) for i in range(x_size)])  13 us
    pallas_call x3, Pallas kernels, attend(): pl.pallas_call(functools.partial(attend_body, first, last, len(keys), hea...  11.2 us
    all_to_all x1, waiting for transfers between devices, spread(): return lax.all_to_all(copies, axes, 0, 0, tiled=False)  11 us
    all_to_all x1, starting transfers between devices, spread(): return lax.all_to_all(copies, axes, 0, 0, tiled=False)  7.87 us
    ppermute x1, starting transfers between devices, layer(): far_quarter = lax.ppermute(quarter, ('zh', 'za', 'zb'), mirror)  7.54 us
  transfers between devices with their start and end apart: 12, of which 4 were waited for; matrix products, arithmetic and copies ran while one was open for 3% of the time, Pallas kernels for 7%

profile of v4, /device:TPU:6, one launch (start us, length us, event | category | flops | bytes accessed | tf_op | source)
XLA Modules:
  0.0 179.2 jit_solution(493483758603452883)
XLA Ops:
  0.0 1.0 copy-done.4
  1.0 0.9 copy-done.5
  1.9 7.7 %collective-permute-start.2 = (bf16[1152,128]{1,0:T(8,128)(2,1)S(1)}, bf16[1152,128]{1,0:T(8,128)(2,1)S(1)}, u32[]{:S(2)}, u32[]{:S(2)}) collective-permute-start(bf16[1152,128]{1,0:T(8,128)(2,1)S(1)} %get-tuple-element.26), channel_id=1, source_target_pairs={{0,128},{128,256},{256,384},{384,0},{1,129},{129,257},{257,385},{3... | collective-permute-start | bytes 884744 | tf_op jit(solution)/shard_map/ppermute | solution.py:261
  9.7 1.9 %collective-permute-start.3 = (bf16[1152,128]{1,0:T(8,128)(2,1)S(1)}, bf16[1152,128]{1,0:T(8,128)(2,1)S(1)}, u32[]{:S(2)}, u32[]{:S(2)}) collective-permute-start(bf16[1152,128]{1,0:T(8,128)(2,1)S(1)} %get-tuple-element.26), channel_id=1, source_target_pairs={{0,384},{128,0},{256,128},{384,256},{1,385},{129,1},{257,129},{385... | collective-permute-start | bytes 884744 | tf_op jit(solution)/shard_map/ppermute | solution.py:261
  11.6 3.4 %collective-permute-start.4 = (bf16[1152,128]{1,0:T(8,128)(2,1)S(1)}, bf16[1152,128]{1,0:T(8,128)(2,1)S(1)}, u32[]{:S(2)}, u32[]{:S(2)}) collective-permute-start(bf16[1152,128]{1,0:T(8,128)(2,1)S(1)} %get-tuple-element.26), channel_id=1, source_target_pairs={{0,256},{128,384},{256,0},{384,128},{1,257},{129,385},{257,1},{385... | collective-permute-start | bytes 884744 | tf_op jit(solution)/shard_map/ppermute | solution.py:261
  15.0 7.5 %collective-permute-start = (bf16[288,128]{1,0:T(8,128)(2,1)S(1)}, bf16[288,128]{1,0:T(8,128)(2,1)S(1)}, u32[]{:S(2)}, u32[]{:S(2)}) collective-permute-start(bf16[288,128]{1,0:T(8,128)(2,1)S(1)} %get-tuple-element.25), channel_id=1, source_target_pairs={{0,92},{4,88},{8,84},{12,80},{16,76},{20,72},{24,68},{28,64},{64,2... | collective-permute-start | bytes 221192 | tf_op jit(solution)/shard_map/ppermute | solution.py:252
  22.7 6.0 %collective-permute-done = bf16[288,128]{1,0:T(8,128)(2,1)S(1)} collective-permute-done((bf16[288,128]{1,0:T(8,128)(2,1)S(1)}, bf16[288,128]{1,0:T(8,128)(2,1)S(1)}, u32[]{:S(2)}, u32[]{:S(2)}) %collective-permute-start) | collective-permute-done | bytes 73760 | tf_op jit(solution)/shard_map/ppermute | solution.py:252
  28.7 1.2 broadcast_in_dim.81
  29.8 7.9 %all-to-all-start = ((bf16[16,288,128]{2,1,0:T(8,128)(2,1)}), bf16[16,288,128]{2,1,0:T(8,128)(2,1)S(1)}, u32[]{:S(2)}, u32[]{:S(2)}) async-start(bf16[16,288,128]{2,1,0:T(8,128)(2,1)} %broadcast_in_dim.81), calls=%async_computation | async-start | bytes 2359296 | tf_op jit(solution)/shard_map/all_to_all | solution.py:23
  37.8 0.6 fusion.9
  39.1 1.2 pad_maximum_fusion.refs_4_
  40.3 2.0 %collective-permute-start.5 = (bf16[4,1152,128]{2,1,0:T(8,128)(2,1)}, bf16[4,1152,128]{2,1,0:T(8,128)(2,1)}, u32[]{:S(2)}, u32[]{:S(2)}) collective-permute-start(bf16[4,1152,128]{2,1,0:T(8,128)(2,1)} %pad_maximum_fusion.refs_4_), channel_id=1, source_target_pairs={{0,32},{32,0},{1,33},{33,1},{2,34},{34,2},{3,35},{35,3},{4,36},{36... | collective-permute-start | bytes 3538952 | tf_op jit(solution)/shard_map/ppermute | solution.py:267
  42.3 0.6 subtract_multiply_fusion
  43.2 11.0 %all-to-all-done = bf16[16,288,128]{2,1,0:T(8,128)(2,1)S(1)} async-done(((bf16[16,288,128]{2,1,0:T(8,128)(2,1)}), bf16[16,288,128]{2,1,0:T(8,128)(2,1)S(1)}, u32[]{:S(2)}, u32[]{:S(2)}) %all-to-all-start) | async-done | bytes 1179680 | tf_op jit(solution)/shard_map/all_to_all | solution.py:23
  54.1 3.5 %all-to-all-start.2 = ((bf16[4,112,512]{2,1,0:T(8,128)(2,1)}), bf16[4,112,512]{2,1,0:T(8,128)(2,1)S(1)}, u32[]{:S(2)}, u32[]{:S(2)}) async-start(bf16[4,112,512]{2,1,0:T(8,128)(2,1)} %bitcast.28), calls=%async_computation.2 | async-start | bytes 917504 | tf_op jit(solution)/shard_map/all_to_all | solution.py:257
  57.6 1.9 %collective-permute-start.1 = (bf16[4,1152,128]{2,1,0:T(8,128)(2,1)S(1)}, bf16[4,1152,128]{2,1,0:T(8,128)(2,1)S(1)}, u32[]{:S(2)}, u32[]{:S(2)}) collective-permute-start(bf16[4,1152,128]{2,1,0:T(8,128)(2,1)S(1)} %bitcast.50), channel_id=1, source_target_pairs={{0,32},{32,0},{1,33},{33,1},{2,34},{34,2},{3,35},{35,3},{4,36},{36... | collective-permute-start | bytes 3538952 | tf_op jit(solution)/shard_map/ppermute | solution.py:268
  61.1 5.1 %attend.3 = (f32[512,128]{1,0:T(8,128)S(1)}, f32[512,128]{1,0:T(8,128)S(1)}, f32[512,512]{1,0:T(8,128)S(1)}) custom-call(bf16[512,512]{1,0:T(8,128)(2,1)S(1)} %bitcast.47, bf16[2,512,128]{2,1,0:T(8,128)(2,1)S(1)} %pad_maximum_fusion.1.refs_1_, s32[2,512]{1,0:T(2,128)S(1)} %pad_add_fusion.refs_2_, s32[2,512]{1,0:T(2,128)S(1)} %pad_add_fusion.1.refs_3_, ...), custom_call_target="tpu_custom_call" | custom-call | flops 2147483648 | bytes 4194304 | tf_op jit(solution)/shard_map/attend/pallas_call | solution.py:163
  66.2 2.3 %attend.4 = (f32[512,128]{1,0:T(8,128)S(1)}, f32[512,128]{1,0:T(8,128)S(1)}, f32[512,512]{1,0:T(8,128)S(1)}) custom-call(bf16[512,512]{1,0:T(8,128)(2,1)S(1)} %bitcast.48, bf16[2,512,128]{2,1,0:T(8,128)(2,1)S(1)} %pad_maximum_fusion.1.refs_1_, s32[1,512]{1,0:T(1,128)S(1)} %bitcast.57, s32[1,512]{1,0:T(1,128)S(1)} %bitcast.58, ...), custom_call_target="tpu_custom_call" | custom-call | flops 1073741824 | bytes 2097152 | tf_op jit(solution)/shard_map/attend/pallas_call | solution.py:163
  68.5 3.9 %attend.5 = bf16[16,128,512]{2,1,0:T(8,128)(2,1)} custom-call(bf16[512,512]{1,0:T(8,128)(2,1)S(1)} %bitcast.49, bf16[2,512,128]{2,1,0:T(8,128)(2,1)S(1)} %pad_maximum_fusion.1.refs_1_, s32[1,512]{1,0:T(1,128)S(1)} %bitcast.55, s32[1,512]{1,0:T(1,128)S(1)} %bitcast.56, bf16[4,1152,128]{2,1,0:T(8,128)(2,1)S(1)} %collective-permute-done.1.refs_4_, ...), custom_call_target="tpu_custom_call" | custom-call | flops 1073741824 | bytes 2097152 | tf_op jit(solution)/shard_map/attend/pallas_call | solution.py:163
  72.4 7.5 %all-to-all-start.1 = ((bf16[16,128,512]{2,1,0:T(8,128)(2,1)}), bf16[16,128,512]{2,1,0:T(8,128)(2,1)S(1)}, u32[]{:S(2)}, u32[]{:S(2)}) async-start(bf16[16,128,512]{2,1,0:T(8,128)(2,1)} %attend.5), calls=%async_computation.1 | async-start | bytes 4194304 | tf_op jit(solution)/shard_map/all_to_all | solution.py:305
  79.8 5.6 %collective-permute-start.6 = (bf16[4,112,512]{2,1,0:T(8,128)(2,1)S(1)}, bf16[4,112,512]{2,1,0:T(8,128)(2,1)S(1)}, u32[]{:S(2)}, u32[]{:S(2)}) collective-permute-start(bf16[4,112,512]{2,1,0:T(8,128)(2,1)S(1)} %all-to-all-done.2.near_ref), channel_id=1, source_target_pairs={{0,64},{64,0},{1,65},{65,1},{2,66},{66,2},{3,67},{67,3},{4,68},{68... | collective-permute-start | bytes 1376264 | tf_op jit(solution)/shard_map/ppermute | solution.py:266
  85.4 1.9 %collective-permute-start.7 = (bf16[4,112,512]{2,1,0:T(8,128)(2,1)S(1)}, bf16[4,112,512]{2,1,0:T(8,128)(2,1)S(1)}, u32[]{:S(2)}, u32[]{:S(2)}) collective-permute-start(bf16[4,112,512]{2,1,0:T(8,128)(2,1)S(1)} %all-to-all-done.2.near_ref), channel_id=1, source_target_pairs={{0,32},{32,0},{1,33},{33,1},{2,34},{34,2},{3,35},{35,3},{4,36},{36... | collective-permute-start | bytes 1376264 | tf_op jit(solution)/shard_map/ppermute | solution.py:269
  87.4 36.3 %collective-permute-done.6.far_ref = bf16[4,112,512]{2,1,0:T(8,128)(2,1)S(1)} collective-permute-done((bf16[4,112,512]{2,1,0:T(8,128)(2,1)S(1)}, bf16[4,112,512]{2,1,0:T(8,128)(2,1)S(1)}, u32[]{:S(2)}, u32[]{:S(2)}) %collective-permute-start.6) | collective-permute-done | bytes 458784 | tf_op jit(solution)/shard_map/ppermute | solution.py:266
  123.7 1.9 %collective-permute-start.8 = (bf16[4,112,512]{2,1,0:T(8,128)(2,1)S(1)}, bf16[4,112,512]{2,1,0:T(8,128)(2,1)S(1)}, u32[]{:S(2)}, u32[]{:S(2)}) collective-permute-start(bf16[4,112,512]{2,1,0:T(8,128)(2,1)S(1)} %collective-permute-done.6.far_ref), channel_id=1, source_target_pairs={{0,32},{32,0},{1,33},{33,1},{2,34},{34,2},{3,35},{35,3},{4,36},{36... | collective-permute-start | bytes 1376264 | tf_op jit(solution)/shard_map/ppermute | solution.py:270
  125.7 1.7 collective-permute-done.8.far_other_ref
  127.4 0.7 join.1.w_ref
  128.1 1.2 copy-done.1
  129.3 1.5 copy-done.2
  130.8 1.1 project.1
  132.0 20.5 %all_to_all.25 = bf16[4,448,128]{2,1,0:T(8,128)(2,1)S(1)} all-to-all(bf16[4,448,128]{2,1,0:T(8,128)(2,1)S(1)} %project.1), channel_id=1, replica_groups=mesh['x'=4,'zh'=2,'core'=2,'za'=2,'zb'=4,'y'=4] {'zb'}, dimensions={0} | all-to-all | bytes 917504 | tf_op jit(solution)/shard_map/all_to_all | solution.py:312
  152.7 25.5 %all_to_all.26 = bf16[32,4,448]{2,1,0:T(4,128)(2,1)S(1)} all-to-all(bf16[32,4,448]{2,1,0:T(4,128)(2,1)S(1)} %reshape.210), channel_id=1, replica_groups=mesh['x'=4,'zh'=2,'core'=2,'za'=2,'zb'=4,'y'=4] {'za','x','y'}, dimensions={0} | all-to-all | bytes 229376 | tf_op jit(solution)/shard_map/all_to_all | solution.py:315
  178.5 0.8 reshape.212
  (47 shorter events, 3.1 us)
Async XLA Ops:
  0.0 60.8 %copy-start = (bf16[4,128,512]{2,1,0:T(8,128)(2,1)S(1)}, bf16[4,128,512]{2,1,0:T(8,128)(2,1)}, u32[]{:S(2)}) copy-start(bf16[4,128,512]{2,1,0:T(8,128)(2,1)} %param.13) | copy-start | bytes 1572868
  0.0 1.0 copy-start.4
  1.0 0.9 copy-start.5
  1.9 37.1 %collective-permute-start.2 = (bf16[1152,128]{1,0:T(8,128)(2,1)S(1)}, bf16[1152,128]{1,0:T(8,128)(2,1)S(1)}, u32[]{:S(2)}, u32[]{:S(2)}) collective-permute-start(bf16[1152,128]{1,0:T(8,128)(2,1)S(1)} %get-tuple-element.26), channel_id=1, source_target_pairs={{0,128},{128,256},{256,384},{384,0},{1,129},{129,257},{257,385},{3... | collective-permute-start | bytes 884744 | tf_op jit(solution)/shard_map/ppermute | solution.py:261
  9.7 29.4 %collective-permute-start.3 = (bf16[1152,128]{1,0:T(8,128)(2,1)S(1)}, bf16[1152,128]{1,0:T(8,128)(2,1)S(1)}, u32[]{:S(2)}, u32[]{:S(2)}) collective-permute-start(bf16[1152,128]{1,0:T(8,128)(2,1)S(1)} %get-tuple-element.26), channel_id=1, source_target_pairs={{0,384},{128,0},{256,128},{384,256},{1,385},{129,1},{257,129},{385... | collective-permute-start | bytes 884744 | tf_op jit(solution)/shard_map/ppermute | solution.py:261
  11.6 27.5 %collective-permute-start.4 = (bf16[1152,128]{1,0:T(8,128)(2,1)S(1)}, bf16[1152,128]{1,0:T(8,128)(2,1)S(1)}, u32[]{:S(2)}, u32[]{:S(2)}) collective-permute-start(bf16[1152,128]{1,0:T(8,128)(2,1)S(1)} %get-tuple-element.26), channel_id=1, source_target_pairs={{0,256},{128,384},{256,0},{384,128},{1,257},{129,385},{257,1},{385... | collective-permute-start | bytes 884744 | tf_op jit(solution)/shard_map/ppermute | solution.py:261
  15.0 13.7 %collective-permute-start = (bf16[288,128]{1,0:T(8,128)(2,1)S(1)}, bf16[288,128]{1,0:T(8,128)(2,1)S(1)}, u32[]{:S(2)}, u32[]{:S(2)}) collective-permute-start(bf16[288,128]{1,0:T(8,128)(2,1)S(1)} %get-tuple-element.25), channel_id=1, source_target_pairs={{0,92},{4,88},{8,84},{12,80},{16,76},{20,72},{24,68},{28,64},{64,2... | collective-permute-start | bytes 221192 | tf_op jit(solution)/shard_map/ppermute | solution.py:252
  29.8 7.9 %copy-start.8 = (s32[16]{0:T(128)S(1)}, s32[16]{0:T(128)}, u32[]{:S(2)}) copy-start(s32[16]{0:T(128)} %param.19) | copy-start | bytes 196
  29.8 7.9 %copy-start.9 = (s32[16]{0:T(128)S(1)}, s32[16]{0:T(128)}, u32[]{:S(2)}) copy-start(s32[16]{0:T(128)} %param.18) | copy-start | bytes 196
  29.8 24.3 %all-to-all-start = ((bf16[16,288,128]{2,1,0:T(8,128)(2,1)}), bf16[16,288,128]{2,1,0:T(8,128)(2,1)S(1)}, u32[]{:S(2)}, u32[]{:S(2)}) async-start(bf16[16,288,128]{2,1,0:T(8,128)(2,1)} %broadcast_in_dim.81), calls=%async_computation | async-start | bytes 2359296 | tf_op jit(solution)/shard_map/all_to_all | solution.py:23
  39.1 3.8 %copy-start.7 = (bf16[128,4,64]{0,2,1:T(8,128)(2,1)S(1)}, bf16[128,4,64]{0,2,1:T(8,128)(2,1)}, u32[]{:S(2)}) copy-start(bf16[128,4,64]{0,2,1:T(8,128)(2,1)} %param.12) | copy-start | bytes 196612
  40.3 20.5 %copy-start.6 = (bf16[128,4,128]{2,1,0:T(4,128)(2,1)S(1)}, bf16[128,4,128]{2,1,0:T(4,128)(2,1)}, u32[]{:S(2)}) copy-start(bf16[128,4,128]{2,1,0:T(4,128)(2,1)} %param.11) | copy-start | bytes 393220
  40.3 20.8 %collective-permute-start.5 = (bf16[4,1152,128]{2,1,0:T(8,128)(2,1)}, bf16[4,1152,128]{2,1,0:T(8,128)(2,1)}, u32[]{:S(2)}, u32[]{:S(2)}) collective-permute-start(bf16[4,1152,128]{2,1,0:T(8,128)(2,1)} %pad_maximum_fusion.refs_4_), channel_id=1, source_target_pairs={{0,32},{32,0},{1,33},{33,1},{2,34},{34,2},{3,35},{35,3},{4,36},{36... | collective-permute-start | bytes 3538952 | tf_op jit(solution)/shard_map/ppermute | solution.py:267
  54.1 18.2 %all-to-all-start.2 = ((bf16[4,112,512]{2,1,0:T(8,128)(2,1)}), bf16[4,112,512]{2,1,0:T(8,128)(2,1)S(1)}, u32[]{:S(2)}, u32[]{:S(2)}) async-start(bf16[4,112,512]{2,1,0:T(8,128)(2,1)} %bitcast.28), calls=%async_computation.2 | async-start | bytes 917504 | tf_op jit(solution)/shard_map/all_to_all | solution.py:257
  57.6 10.8 %collective-permute-start.1 = (bf16[4,1152,128]{2,1,0:T(8,128)(2,1)S(1)}, bf16[4,1152,128]{2,1,0:T(8,128)(2,1)S(1)}, u32[]{:S(2)}, u32[]{:S(2)}) collective-permute-start(bf16[4,1152,128]{2,1,0:T(8,128)(2,1)S(1)} %bitcast.50), channel_id=1, source_target_pairs={{0,32},{32,0},{1,33},{33,1},{2,34},{34,2},{3,35},{35,3},{4,36},{36... | collective-permute-start | bytes 3538952 | tf_op jit(solution)/shard_map/ppermute | solution.py:268
  66.2 2.3 %copy-start.3 = (bf16[4,512,128]{2,1,0:T(8,128)(2,1)S(1)}, bf16[4,512,128]{2,1,0:T(8,128)(2,1)}, u32[]{:S(2)}) copy-start(bf16[4,512,128]{2,1,0:T(8,128)(2,1)} %refs_8_.1) | copy-start | bytes 1572868
  72.4 57.0 %all-to-all-start.1 = ((bf16[16,128,512]{2,1,0:T(8,128)(2,1)}), bf16[16,128,512]{2,1,0:T(8,128)(2,1)S(1)}, u32[]{:S(2)}, u32[]{:S(2)}) async-start(bf16[16,128,512]{2,1,0:T(8,128)(2,1)} %attend.5), calls=%async_computation.1 | async-start | bytes 4194304 | tf_op jit(solution)/shard_map/all_to_all | solution.py:305
  79.8 43.9 %collective-permute-start.6 = (bf16[4,112,512]{2,1,0:T(8,128)(2,1)S(1)}, bf16[4,112,512]{2,1,0:T(8,128)(2,1)S(1)}, u32[]{:S(2)}, u32[]{:S(2)}) collective-permute-start(bf16[4,112,512]{2,1,0:T(8,128)(2,1)S(1)} %all-to-all-done.2.near_ref), channel_id=1, source_target_pairs={{0,64},{64,0},{1,65},{65,1},{2,66},{66,2},{3,67},{67,3},{4,68},{68... | collective-permute-start | bytes 1376264 | tf_op jit(solution)/shard_map/ppermute | solution.py:266
  85.4 40.3 %collective-permute-start.7 = (bf16[4,112,512]{2,1,0:T(8,128)(2,1)S(1)}, bf16[4,112,512]{2,1,0:T(8,128)(2,1)S(1)}, u32[]{:S(2)}, u32[]{:S(2)}) collective-permute-start(bf16[4,112,512]{2,1,0:T(8,128)(2,1)S(1)} %all-to-all-done.2.near_ref), channel_id=1, source_target_pairs={{0,32},{32,0},{1,33},{33,1},{2,34},{34,2},{3,35},{35,3},{4,36},{36... | collective-permute-start | bytes 1376264 | tf_op jit(solution)/shard_map/ppermute | solution.py:269
  123.7 3.7 %collective-permute-start.8 = (bf16[4,112,512]{2,1,0:T(8,128)(2,1)S(1)}, bf16[4,112,512]{2,1,0:T(8,128)(2,1)S(1)}, u32[]{:S(2)}, u32[]{:S(2)}) collective-permute-start(bf16[4,112,512]{2,1,0:T(8,128)(2,1)S(1)} %collective-permute-done.6.far_ref), channel_id=1, source_target_pairs={{0,32},{32,0},{1,33},{33,1},{2,34},{34,2},{3,35},{35,3},{4,36},{36... | collective-permute-start | bytes 1376264 | tf_op jit(solution)/shard_map/ppermute | solution.py:270
  128.1 1.2 copy-start.1
  129.3 1.5 copy-start.2
